TPU v7x, 256 devices: a whole 4x4x8 slice. The times are simulated.
256 devices in a mesh: expert: 32 (over y, z), ctx: 8 (over x, core).
Axes of the slice: x: 4, y: 4, z: 8, core: 2. Of those that a mesh axis runs over, the one named last changes fastest.
Arguments:
- tokens: bfloat16 [4096, 4096], P('expert', 'ctx'), may hold values from -6 to 6
- grad_out: bfloat16 [4096, 4096], P('expert', 'ctx'), may hold values from -1.5 to 1.5
- expert_ids: int32 [4096, 8], P('expert'), may hold values from 0 to 63, all different within a row; in each aligned block of 128 rows (0 to 127, 128 to 255, ...) at most 18 rows name the same one
- gate_probs: float32 [4096, 8], P('expert'), may hold values from 0.05 to 1
- gate_weight: bfloat16 [64, 1536, 4096], P('expert', 'ctx'), may hold values from -0.09375 to 0.09375
- up_weight: bfloat16 [64, 1536, 4096], P('expert', 'ctx'), may hold values from -0.09375 to 0.09375
- down_weight: bfloat16 [64, 1536, 4096], P('expert', 'ctx'), may hold values from -0.15625 to 0.15625
Outputs:
- grad_tokens: bfloat16 [4096, 4096], P('expert', 'ctx')
- grad_gates: bfloat16 [4096, 8], P('expert')
Inputs may be any that keep to these rules, and one draw needn't show every extreme that they name: `expert_ids`: each row names 8 different experts. Within the 128 rows of one index of expert (aligned blocks), no expert is named more than 18 times, and in every draw some expert is named exactly 18 times in some block.
All inputs are finite; a program needn't handle non-finite values.
Results may differ from a plain program's by a relative error of at most 0.014.
Values may be sent and summed in bfloat16 or wider, within the bound.
A program may use at most 128 MiB of HBM per device.

v0:
```python
import jax
import jax.numpy as jnp
from jax import lax
from jax.sharding import PartitionSpec as P


def route_tables(expert_ids, experts, capacity):
    tok_count, top_count = expert_ids.shape
    flat_ids = expert_ids.reshape(-1)
    one_hot = (flat_ids[:, None] == jnp.arange(experts, dtype=jnp.int32)[None, :]).astype(jnp.int32)
    earlier = jnp.cumsum(one_hot, axis=0) - one_hot
    slot_rank = jnp.sum(earlier * one_hot, axis=1)
    slot_index = (flat_ids * capacity + slot_rank).reshape(tok_count, top_count)
    matches = (
        slot_index[:, :, None] == jnp.arange(experts * capacity, dtype=jnp.int32)[None, None, :]
    )
    placing = jnp.any(matches, axis=1).astype(jnp.bfloat16)
    return (slot_index, placing)


def body(tokens, grad_out, expert_ids, gate_probs, gate_weight, up_weight, down_weight):
    tok_count, top_count = expert_ids.shape
    groups = lax.axis_size("expert")
    local_count = gate_weight.shape[0]
    experts = local_count * groups
    capacity = tok_count * top_count // experts + max(1, tok_count * top_count // (8 * experts))
    full_width = gate_weight.shape[2]
    slot_index, placing = route_tables(expert_ids, experts, capacity)
    sent_rows = jnp.einsum("tc,td->cd", placing, tokens, preferred_element_type=jnp.float32).astype(
        jnp.bfloat16
    )
    sent_grads = jnp.einsum(
        "tc,td->cd", placing, grad_out, preferred_element_type=jnp.float32
    ).astype(jnp.bfloat16)
    sent_rows = sent_rows.reshape(groups, local_count * capacity, -1)
    sent_grads = sent_grads.reshape(groups, local_count * capacity, -1)
    got_rows, got_grads = (
        lax.all_to_all(sent_rows, "expert", split_axis=0, concat_axis=0, tiled=True),
        lax.all_to_all(sent_grads, "expert", split_axis=0, concat_axis=0, tiled=True),
    )
    rows_in, rows_grad = (
        lax.all_gather(got_rows, "ctx", axis=2, tiled=True),
        lax.all_gather(got_grads, "ctx", axis=2, tiled=True),
    )
    rows_in = rows_in.reshape(groups, local_count, capacity, full_width)
    rows_grad = rows_grad.reshape(groups, local_count, capacity, full_width)
    pre_gate = jnp.einsum(
        "secd,efd->secf", rows_in, gate_weight, preferred_element_type=jnp.float32
    )
    pre_up = jnp.einsum("secd,efd->secf", rows_in, up_weight, preferred_element_type=jnp.float32)
    grad_hidden = jnp.einsum(
        "secd,efd->secf", rows_grad, down_weight, preferred_element_type=jnp.float32
    )
    sigmoid_gate = jax.nn.sigmoid(pre_gate)
    activated = pre_gate * sigmoid_gate
    gate_score = jnp.sum(activated * pre_up * grad_hidden, axis=3)
    grad_pre_gate = (
        grad_hidden * pre_up * sigmoid_gate * (1.0 + pre_gate * (1.0 - sigmoid_gate))
    ).astype(jnp.bfloat16)
    grad_pre_up = (grad_hidden * activated).astype(jnp.bfloat16)
    partials = jnp.einsum(
        "secf,efd->secd", grad_pre_gate, gate_weight, preferred_element_type=jnp.float32
    )
    partials = partials + jnp.einsum(
        "secf,efd->secd", grad_pre_up, up_weight, preferred_element_type=jnp.float32
    )
    block_terms = partials.astype(jnp.bfloat16)
    summed = lax.psum_scatter(block_terms, "ctx", scatter_dimension=3, tiled=True).astype(
        jnp.float32
    )
    gate_total = lax.psum(gate_score, "ctx")
    back_rows = summed.astype(jnp.bfloat16).reshape(groups, local_count * capacity, -1)
    back_scores = gate_total.astype(jnp.bfloat16).reshape(groups, local_count * capacity)
    home_rows, home_scores = (
        lax.all_to_all(back_rows, "expert", split_axis=0, concat_axis=0, tiled=True),
        lax.all_to_all(back_scores, "expert", split_axis=0, concat_axis=0, tiled=True),
    )
    contribution = home_rows.reshape(experts * capacity, -1)
    picked = jnp.take(contribution, slot_index.reshape(-1), axis=0).reshape(
        tok_count, top_count, -1
    )
    grad_tokens = jnp.sum(gate_probs[:, :, None] * picked.astype(jnp.float32), axis=1)
    grad_gates = jnp.take(home_scores.reshape(-1), slot_index.reshape(-1)).reshape(
        tok_count, top_count
    )
    return (grad_tokens.astype(jnp.bfloat16), grad_gates)


def solution(mesh):
    in_specs = (
        P("expert", "ctx"),
        P("expert", "ctx"),
        P("expert", None),
        P("expert", None),
        P("expert", "ctx", None),
        P("expert", "ctx", None),
        P("expert", "ctx", None),
    )
    out_specs = (P("expert", "ctx"), P("expert", None))
    return jax.shard_map(body, mesh=mesh, in_specs=in_specs, out_specs=out_specs, check_vma=False)
```

profile of v0, /device:TPU:32, one launch (start us, length us, event | category | flops | bytes accessed | tf_op | source)
XLA Modules:
  0.0 384.7 jit_solution(9494247804040030120)
XLA Ops:
  7.2 0.0 copy-start
  7.2 0.0 all-gather.5.cloned.1.call-start
  7.2 0.9 copy.48
  8.2 0.1 eq.39
  8.3 0.1 reshape.102
  8.3 0.7 fusion.25
  9.1 30.8 %reduce-window.6 = s32[64,8,128]{2,1,0:T(8,128)S(1)} reduce-window(s32[64,8,128]{2,1,0:T(8,128)} %fusion.25, s32[]{:T(128)} %constant.23.clone.1), window={size=1x1x128 pad=0_0x0_0x127_0}, to_apply=%region_0.0 | reduce-window | flops 8323072 | bytes 524292 | tf_op jit(solution)/shard_map/reduce-window
  39.9 0.8 slice.12
  40.7 1.1 copy.51
  41.8 0.1 copy.52
  41.9 0.1 broadcast_add_fusion
  42.1 0.1 fusion.24
  42.1 0.1 reduce_sum.32
  42.3 1.5 fusion.1
  43.7 2.5 convolution_convert_fusion
  46.2 2.9 reshape.106
  49.1 46.2 %all_to_all.24 = bf16[32,36,512]{2,1,0:T(8,128)(2,1)} all-to-all(bf16[32,36,512]{2,1,0:T(8,128)(2,1)} %reshape.106), channel_id=1, replica_groups=mesh['expert'=32,'ctx'=8] {'expert'}, dimensions={0} | all-to-all | bytes 2359296 | tf_op jit(solution)/shard_map/all_to_all | solution.py:38
  95.3 0.0 all-gather.5.cloned.1.call-update
  95.3 0.0 all-gather.3.cloned.1.call-start
  95.4 2.4 convolution_convert_fusion.1
  97.8 2.9 reshape.104
  100.8 39.2 %all_to_all.25 = bf16[32,36,512]{2,1,0:T(8,128)(2,1)} all-to-all(bf16[32,36,512]{2,1,0:T(8,128)(2,1)} %reshape.104), channel_id=1, replica_groups=mesh['expert'=32,'ctx'=8] {'expert'}, dimensions={0} | all-to-all | bytes 2359296 | tf_op jit(solution)/shard_map/all_to_all | solution.py:39
  140.0 0.0 all-gather.3.cloned.1.call-update
  140.0 0.2 reduce-scatter.2.cloned.1.call-start
  140.3 12.1 %all-gather.5.cloned.1.call-done = bf16[32,36,4096]{2,1,0:T(8,128)(2,1)} async-done(((bf16[32,36,512]{2,1,0:T(8,128)(2,1)}), bf16[32,36,4096]{2,1,0:T(8,128)(2,1)}) %all-gather.5.cloned.1.call-update) | async-done | bytes 9437200 | tf_op jit(solution)/shard_map/all_gather | solution.py:42
  152.3 12.8 %copy.54 = bf16[32,36,4096]{2,0,1:T(8,128)(2,1)} copy(bf16[32,36,4096]{2,1,0:T(8,128)(2,1)} %all-gather.5.cloned.1.call-done) | data formatting | bytes 18874368 | tf_op jit(solution)/shard_map/all_gather | solution.py:42
  165.1 0.0 copy-done
  165.1 0.0 copy-start.2
  165.1 0.0 copy-start.5
  165.1 8.6 %fusion.17 = f32[32,2,18,192]{3,0,2,1:T(8,128)} fusion(bf16[32,2,18,4096]{3,0,2,1:T(8,128)(2,1)} %bitcast.72, bf16[2,192,4096]{2,1,0:T(8,128)(2,1)S(1)} %copy-done), kind=kOutput, calls=%fused_computation.20 | convolution fusion | flops 1811939328 | bytes 13467648 | tf_op jit(solution)/shard_map/secd,efd->secf/dot_general | solution.py:47
  173.7 0.0 copy-done.2
  173.7 0.8 copy-done.5
  174.5 3.6 fusion.11
  178.1 37.4 %all-gather.3.cloned.1.call-done = bf16[32,36,4096]{2,1,0:T(8,128)(2,1)} async-done(((bf16[32,36,512]{2,1,0:T(8,128)(2,1)}), bf16[32,36,4096]{2,1,0:T(8,128)(2,1)}) %all-gather.3.cloned.1.call-update) | async-done | bytes 9437200 | tf_op jit(solution)/shard_map/all_gather | solution.py:43
  215.5 13.0 %copy.53 = bf16[32,36,4096]{2,0,1:T(8,128)(2,1)} copy(bf16[32,36,4096]{2,1,0:T(8,128)(2,1)} %all-gather.3.cloned.1.call-done) | data formatting | bytes 18874368 | tf_op jit(solution)/shard_map/all_gather | solution.py:43
  228.5 0.0 copy-start.3
  228.5 8.3 %multiply_reduce_fusion.1 = (f32[32,2,18]{0,2,1:T(8,128)S(1)}, f32[32,2,18,192]{3,0,2,1:T(8,128)S(1)}) fusion(f32[32,2,18,192]{3,0,2,1:T(8,128)} %fusion.11, f32[32,2,18,192]{3,0,2,1:T(8,128)} %fusion.17, bf16[32,2,18,4096]{3,0,2,1:T(8,128)(2,1)} %bitcast.71, bf16[2,192,4096]{2,1,0:T(8,128)(2,1)} %param.13), kind=kOutput, calls=%fused_computation.21 | convolution fusion | flops 1813486464 | bytes 15241728 | tf_op jit(solution)/shard_map/secd,efd->secf/dot_general | solution.py:51
  236.8 0.0 copy-start.4
  236.8 1.0 copy-done.4
  237.8 0.0 copy-done.3
  237.8 0.0 copy-done.6
  237.8 8.0 %fusion.2 = f32[2,32,18,4096]{3,1,2,0:T(8,128)} fusion(bf16[2,192,4096]{2,1,0:T(8,128)(2,1)S(1)} %copy-done, f32[32,2,18,192]{3,0,2,1:T(8,128)S(1)} %copy-done.3, f32[32,2,18,192]{3,0,2,1:T(8,128)S(1)} %get-tuple-element.15, f32[32,2,18,192]{3,0,2,1:T(8,128)S(1)} %copy-done.6), kind=kOutput, calls=%fused_computation.6 | convolution fusion | flops 1814151168 | bytes 24674304 | tf_op jit(solution)/shard_map/secf,efd->secd/dot_general | solution.py:61
  245.9 14.4 %fusion = bf16[32,2,18,4096]{3,0,2,1:T(8,128)(2,1)} fusion(f32[2,32,18,4096]{3,1,2,0:T(8,128)} %fusion.2, bf16[2,192,4096]{2,1,0:T(8,128)(2,1)} %param.12, f32[32,2,18,192]{3,0,2,1:T(8,128)} %copy-done.4, f32[32,2,18,192]{3,0,2,1:T(8,128)} %fusion.17), kind=kOutput, calls=%fused_computation.3 | convolution fusion | flops 1822703616 | bytes 33226752 | tf_op jit(solution)/shard_map/secf,efd->secd/dot_general | solution.py:64
  260.3 0.0 reduce-scatter.2.cloned.1.call-update
  260.3 24.8 %psum.7 = bf16[32,2,18]{0,2,1:T(8,128)(2,1)S(1)} all-reduce(f32[32,2,18]{0,2,1:T(8,128)S(1)} %get-tuple-element.14), channel_id=1, replica_groups=mesh['expert'=32,'ctx'=8] {'ctx'}, use_global_device_ids=true, to_apply=%region_7.8 | all-reduce | flops 1152 | bytes 6912 | tf_op jit(solution)/shard_map/psum | solution.py:71
  285.1 0.7 copy.56
  285.8 10.1 %all-to-all-start.3 = ((bf16[32,1,36]{2,1,0:T(2,128)(2,1)}), bf16[32,1,36]{2,1,0:T(2,128)(2,1)S(1)}, u32[]{:S(2)}, u32[]{:S(2)}) async-start(bf16[32,1,36]{2,1,0:T(2,128)(2,1)} %copy.56), calls=%async_computation.4 | async-start | bytes 32768 | tf_op jit(solution)/shard_map/all_to_all | solution.py:76
  295.9 25.0 %reduce-scatter.2.cloned.1.call-done = bf16[32,2,18,512]{3,0,2,1:T(8,128)(2,1)} async-done(((bf16[32,2,18,4096]{3,0,2,1:T(8,128)(2,1)}), bf16[32,2,18,512]{3,0,2,1:T(8,128)(2,1)}) %reduce-scatter.2.cloned.1.call-update) | async-done | bytes 1179664 | tf_op jit(solution)/shard_map/reduce_scatter | solution.py:68
  320.9 3.0 copy.55
  323.9 0.0 all-to-all-done.3
  323.9 10.5 %all-to-all-start.2 = ((bf16[32,36,512]{2,1,0:T(8,128)(2,1)}), bf16[32,36,512]{2,1,0:T(8,128)(2,1)S(1)}, u32[]{:S(2)}, u32[]{:S(2)}) async-start(bf16[32,36,512]{2,1,0:T(8,128)(2,1)} %copy.55), calls=%async_computation.3 | async-start | bytes 2621440 | tf_op jit(solution)/shard_map/all_to_all | solution.py:75
  334.4 0.0 copy-done.7
  334.4 0.1 copy.47
  334.5 0.1 mul.67
  334.6 0.1 reduce
  334.7 0.1 reshape.110
  334.8 6.8 %gather_fusion.1 = bf16[1024]{0:T(1024)(128)(2,1)S(1)} fusion(bf16[1152]{0:T(1024)(128)(2,1)S(1)} %reshape.110, s32[1024]{0:T(1024)S(1)} %broadcast_clamp_fusion), kind=kCustom, calls=%fused_computation.1 | custom fusion | bytes 8192 | tf_op jit(solution)/shard_map/jit(_take)/gather | solution.py:83
  341.6 0.1 gather.15
  341.7 0.7 copy.57
  342.4 25.3 %all-to-all-done.2 = bf16[32,36,512]{2,1,0:T(8,128)(2,1)S(1)} async-done(((bf16[32,36,512]{2,1,0:T(8,128)(2,1)}), bf16[32,36,512]{2,1,0:T(8,128)(2,1)S(1)}, u32[]{:S(2)}, u32[]{:S(2)}) %all-to-all-start.2) | async-done | bytes 1179680 | tf_op jit(solution)/shard_map/all_to_all | solution.py:75
  367.7 1.1 reshape.109
  368.8 6.7 %gather_fusion = bf16[1024,512]{1,0:T(8,128)(2,1)} fusion(bf16[1152,512]{1,0:T(8,128)(2,1)} %reshape.109, s32[1024]{0:T(1024)S(1)} %broadcast_clamp_fusion), kind=kCustom, calls=%fused_computation | custom fusion | bytes 2101248 | tf_op jit(solution)/shard_map/jit(_take)/gather | solution.py:79
  375.5 2.7 multiply_reduce_fusion
  378.2 0.0 copy-done.1
  (10 shorter events, 0.1 us)
Async XLA Ops:
  7.2 158.0 %copy-start = (bf16[2,192,4096]{2,1,0:T(8,128)(2,1)S(1)}, bf16[2,192,4096]{2,1,0:T(8,128)(2,1)}, u32[]{:S(2)}) copy-start(bf16[2,192,4096]{2,1,0:T(8,128)(2,1)} %param.11) | copy-start | bytes 9437188
  7.2 145.2 %all-gather.5.cloned.1.call-start = ((), (), s32[]{:S(2)}) async-start(), calls=%async_computation.6 | async-start | bytes 11796480 | tf_op jit(solution)/shard_map/all_gather | solution.py:42
  95.3 120.2 %all-gather.3.cloned.1.call-start = ((), (), s32[]{:S(2)}) async-start(), calls=%async_computation.5 | async-start | bytes 11796480 | tf_op jit(solution)/shard_map/all_gather | solution.py:43
  140.0 180.9 %reduce-scatter.2.cloned.1.call-start = ((), (), s32[]{:S(2)}) async-start(), calls=%async_computation.7 | async-start | bytes 10616832 | tf_op jit(solution)/shard_map/reduce_scatter | solution.py:68
  165.1 8.6 %copy-start.2 = (bf16[32,36,4096]{2,0,1:T(8,128)(2,1)S(1)}, bf16[32,36,4096]{2,0,1:T(8,128)(2,1)}, u32[]{:S(2)}) copy-start(bf16[32,36,4096]{2,0,1:T(8,128)(2,1)} %copy.54) | copy-start | bytes 28311556
  165.1 9.4 %copy-start.5 = (bf16[2,192,4096]{2,1,0:T(8,128)(2,1)S(1)}, bf16[2,192,4096]{2,1,0:T(8,128)(2,1)}, u32[]{:S(2)}) copy-start(bf16[2,192,4096]{2,1,0:T(8,128)(2,1)} %param.12) | copy-start | bytes 9437188
  228.5 9.3 %copy-start.3 = (f32[32,2,18,192]{3,0,2,1:T(8,128)S(1)}, f32[32,2,18,192]{3,0,2,1:T(8,128)}, u32[]{:S(2)}) copy-start(f32[32,2,18,192]{3,0,2,1:T(8,128)} %fusion.17) | copy-start | bytes 2654212
  228.5 9.3 %copy-start.6 = (f32[32,2,18,192]{3,0,2,1:T(8,128)S(1)}, f32[32,2,18,192]{3,0,2,1:T(8,128)}, u32[]{:S(2)}) copy-start(f32[32,2,18,192]{3,0,2,1:T(8,128)} %fusion.11) | copy-start | bytes 2654212
  236.8 1.0 copy-start.4
  285.8 38.0 %all-to-all-start.3 = ((bf16[32,1,36]{2,1,0:T(2,128)(2,1)}), bf16[32,1,36]{2,1,0:T(2,128)(2,1)S(1)}, u32[]{:S(2)}, u32[]{:S(2)}) async-start(bf16[32,1,36]{2,1,0:T(2,128)(2,1)} %copy.56), calls=%async_computation.4 | async-start | bytes 32768 | tf_op jit(solution)/shard_map/all_to_all | solution.py:76
  323.9 10.5 %copy-start.7 = (f32[128,8]{0,1:T(8,128)S(1)}, f32[128,8]{0,1:T(8,128)}, u32[]{:S(2)}) copy-start(f32[128,8]{0,1:T(8,128)} %param.10) | copy-start | bytes 12292
  323.9 43.8 %all-to-all-start.2 = ((bf16[32,36,512]{2,1,0:T(8,128)(2,1)}), bf16[32,36,512]{2,1,0:T(8,128)(2,1)S(1)}, u32[]{:S(2)}, u32[]{:S(2)}) async-start(bf16[32,36,512]{2,1,0:T(8,128)(2,1)} %copy.55), calls=%async_computation.3 | async-start | bytes 2621440 | tf_op jit(solution)/shard_map/all_to_all | solution.py:75
  368.8 9.4 %copy-start.1 = (bf16[2,192,4096]{2,1,0:T(8,128)(2,1)S(1)}, bf16[2,192,4096]{2,1,0:T(8,128)(2,1)}, u32[]{:S(2)}) copy-start(bf16[2,192,4096]{2,1,0:T(8,128)(2,1)} %param.11) | copy-start | bytes 9437188
Sparse Core Ops, SparseCore 0:
  95.5 56.8 all-gather.4
  154.2 61.2 all-gather.2
  260.4 60.4 reduce-scatter.1
where the time goes:
time: 387 us; the launch traced here: 385 us
  blocking collectives  110 us (28%)
  waiting for transfers between devices  99.8 us (26%)
  local copies, waits for them, and re-layouts  56 us (14%)
  matrix products  47.8 us (12%)
  other arithmetic  36.1 us (9%)
  starting transfers between devices  20.9 us (5%)
  between operations  13.9 us (4%)
    all_to_all x1, blocking collectives, body(): lax.all_to_all(sent_rows, 'expert', split_axis=0, concat_axis=0, tiled=True)  46.2 us
    all_to_all x1, blocking collectives, body(): lax.all_to_all(sent_grads, 'expert', split_axis=0, concat_axis=0, tiled=T...  39.2 us
    all_gather x1, waiting for transfers between devices, body(): lax.all_gather(got_grads, 'ctx', axis=2, tiled=True)  37.4 us
    another operation x3, other arithmetic  31 us
    all_to_all x1, waiting for transfers between devices, body(): lax.all_to_all(back_rows, 'expert', split_axis=0, concat_axis=0, tiled=True)  25.3 us
    reduce_scatter x1, waiting for transfers between devices, body(): lax.psum_scatter(block_terms, 'ctx', scatter_dimension=3, tiled=True)  25 us
    psum x1, blocking collectives, body(): gate_total = lax.psum(gate_score, 'ctx')  24.8 us
    dot_general x1, matrix products, body(): jnp.einsum('secf,efd->secd', grad_pre_up, up_weight, preferred_element_ty...  14.4 us
  transfers between devices with their start and end apart: 5, of which 4 were waited for; matrix products, arithmetic and copies ran while one was open for 11% of the time, Pallas kernels for 0%

commit v1 on v0

v1 whole, which is shorter than its diff:
```python
import jax
import jax.numpy as jnp
from jax import lax
from jax.experimental import pallas as pl
from jax.experimental.pallas import tpu as pltpu
from jax.sharding import PartitionSpec as P

MESH = pl.DeviceIdType.MESH
NY, NZ, NX = 4, 8, 4
CAP, TOK, TOP = 18, 128, 8
R = NZ * CAP
FS, FFL, NF = 512, 192, 8
D = FS * NF
Q = NY * 2
BF, F32 = jnp.bfloat16, jnp.float32


def rc(src, dst, ss, rs, dev):
    return pltpu.make_async_remote_copy(
        src_ref=src, dst_ref=dst, send_sem=ss, recv_sem=rs, device_id=dev, device_id_type=MESH
    )


def kernel(
    tok, grad, meta, wg, wu, wd, out, gg,
    XB, MB, KEY, WT, PLB, GB, RB, WV, PB, PX, RA, RM, FB, YB, T, ZS, ZR,
    SC, SCR, SCT, YSC, SE, ZSC,
    ls, ws, zs, zv, ms, mv, ys, yv, xs, xv, ps, pv, pxs, pxv, as_, av, rs, rv, rys, ryv, zrs, zrv,
    scs, scv, sys_, syv, szs, szv,
):
    me_e, me_c = lax.axis_index("expert"), lax.axis_index("ctx")
    y, z = me_e // NZ, me_e % NZ
    x, c = me_c // 2, me_c % 2

    def xdev(dx):
        return {"ctx": ((x + dx) % NX) * 2 + c}

    partner = {"ctx": x * 2 + 1 - c}

    def ydev(dy):
        return {"expert": ((y + dy) % NY) * NZ + z}

    def zdev(dz):
        return {"expert": y * NZ + (z + dz) % NZ}

    def cdev(k):
        return {"ctx": (me_c + k) % NF}

    loads = [
        pltpu.make_async_copy(tok, XB.at[0, 0], ls.at[0]),
        pltpu.make_async_copy(grad, XB.at[0, 1], ls.at[1]),
        pltpu.make_async_copy(meta, MB.at[0], ls.at[2]),
    ]
    for cp in loads:
        cp.start()

    barrier = pltpu.get_barrier_semaphore()
    peers = [cdev(k) for k in range(1, NF)] + [ydev(k) for k in range(1, NY)]
    peers += [zdev(k) for k in range(1, NZ)]
    for peer in peers:
        pl.semaphore_signal(barrier, inc=1, device_id=peer, device_id_type=MESH)
    pl.semaphore_wait(barrier, len(peers))
    for cp in loads:
        cp.wait()

    def zx(way, s):
        if way == 0:
            si, di, dev, part = (NZ - (s - 1)) % NZ, NZ - s, zdev(1), 0
        else:
            si, di, dev, part = s - 1, s, zdev(NZ - 1), 1
        if s < NZ // 2:
            return rc(XB.at[si], XB.at[di], zs.at[way, s - 1], zv.at[way, s - 1], dev)
        return rc(XB.at[si, part], XB.at[di, part], zs.at[way, s - 1], zv.at[way, s - 1], dev)

    def zm(way, s):
        if way == 0:
            si, di, dev = (NZ - (s - 1)) % NZ, NZ - s, zdev(1)
        else:
            si, di, dev = s - 1, s, zdev(NZ - 1)
        return rc(MB.at[si], MB.at[di], ms.at[way, s - 1], mv.at[way, s - 1], dev)

    lane = lax.broadcasted_iota(jnp.int32, (TOK, TOK), 1)
    sub = lax.broadcasted_iota(jnp.int32, (TOK, TOK), 0)
    before = (sub < lane).astype(BF)
    erow = lax.broadcasted_iota(jnp.int32, (8, TOK), 0)
    dyrow = erow // 2
    expert = (2 * (((y + dyrow) % NY) * NZ + z) + (erow - 2 * dyrow)).astype(F32)

    def key(d):
        member = jnp.zeros((8, TOK), F32)
        weight = jnp.zeros((8, TOK), F32)
        for k in range(TOP):
            hit = jnp.broadcast_to(MB[d, k : k + 1, :], (8, TOK)) == expert
            member = member + jnp.where(hit, 1.0, 0.0)
            prob = jnp.broadcast_to(MB[d, TOP + k : TOP + k + 1, :], (8, TOK))
            weight = weight + jnp.where(hit, prob, 0.0)
        rank = jnp.dot(member.astype(BF), before, preferred_element_type=F32)
        slot = jnp.where(member > 0.5, rank + float(d * CAP), -1.0)
        for e in range(8):
            KEY[e, :, d * TOK : (d + 1) * TOK] = slot[e : e + 1]
            WT[e, :, d * TOK : (d + 1) * TOK] = weight[e : e + 1]

    half = NZ // 2
    for way in range(2):
        zm(way, 1).start()
        zx(way, 1).start()

    def wload(j, f, m):
        xo = (0, NX - 1, 1, 2)[f % 4]
        ctx = ((x + xo) % NX) * 2 + (c if f < 4 else 1 - c)
        src = (wg, wu, wd)[m].at[j, :, pl.ds(pl.multiple_of(ctx * FS, FS), FS)]
        dst = WV.at[j, pl.ds(m * FFL, FFL), pl.ds(f * FS, FS)]
        return pltpu.make_async_copy(src, dst, ws.at[j, f, m])

    wloads = [wload(j, f, m) for j in range(2) for f in range(NF) for m in range(3)]
    for cp in wloads:
        cp.start()

    key(0)
    for s in range(1, half + 1):
        for way in range(2):
            if s < half or way == 0:
                zm(way, s).wait_recv()
                if s + 1 < half or (s + 1 == half and way == 0):
                    zm(way, s + 1).start()
            zx(way, s).wait_recv()
            if s < half:
                zx(way, s + 1).start()
        key(NZ - s)
        if s < half:
            key(s)

    rowid = lax.broadcasted_iota(jnp.int32, (R, NZ * TOK), 0).astype(F32)

    def place(e):
        hit = jnp.broadcast_to(KEY[e], (R, NZ * TOK)) == rowid
        PLB[e] = jnp.where(hit, 1.0, 0.0).astype(BF)

    def gather(e, a):
        slab = XB[:, a].reshape(NZ * TOK, FS)
        return jnp.dot(PLB[e], slab, preferred_element_type=F32).astype(BF)

    def own(q):
        return RB.at[q, :, :, pl.ds(0, FS)]

    def fsl(q, f):
        return RB.at[q, :, :, pl.ds(f * FS, FS)]

    def xr(q):
        return rc(own(q), fsl(q, 1), xs.at[q, 0], xv.at[q, 0], xdev(1))

    def xl(q):
        return rc(own(q), fsl(q, 2), xs.at[q, 1], xv.at[q, 1], xdev(NX - 1))

    def xt(q):
        return rc(
            RB.at[q, 0, :, pl.ds(FS, FS)], RB.at[q, 0, :, pl.ds(3 * FS, FS)],
            xs.at[q, 2], xv.at[q, 2], xdev(1),
        )

    def xg(q):
        return rc(
            RB.at[q, 1, :, pl.ds(2 * FS, FS)], RB.at[q, 1, :, pl.ds(3 * FS, FS)],
            xs.at[q, 3], xv.at[q, 3], xdev(NX - 1),
        )

    def pp(q, f):
        return rc(fsl(q, f), fsl(q, 4 + f), ps.at[q, f], pv.at[q, f], partner)

    def yc(q):
        return rc(GB.at[q - 2], own(q), ys.at[q - 2], yv.at[q - 2], ydev(NY - q // 2))

    def send_own(q):
        xr(q).start()
        xl(q).start()
        pp(q, 0).start()

    @pl.loop(0, 2)
    def _(q):
        place(q)
        for a in range(2):
            RB[q, a, :, 0:FS] = gather(q, a)
        send_own(q)

    @pl.loop(2, Q)
    def _(q):
        e = ((NY - q // 2) % NY) * 2 + q % 2
        place(e)
        for a in range(2):
            GB[q - 2, a] = gather(e, a)
        yc(q).start()

    for cp in wloads:
        cp.wait()
    for d in range(NZ):
        T[d] = jnp.zeros((TOK, FS), F32)

    nt = (((1,), (1,)), ((), ()))
    tn = (((0,), (0,)), ((), ()))

    def px(q):
        return rc(PB.at[q, pl.ds(4, 4)], PX.at[q], pxs.at[q], pxv.at[q], partner)

    def ra(q, w):
        return rc(
            PB.at[q, 3, :, pl.ds(w * (FS // 2), FS // 2)], RA.at[q, w],
            as_.at[q, w], av.at[q, w], xdev(1 if w == 0 else NX - 1),
        )

    def rm(q, w):
        return rc(
            PB.at[q, 2 - w], RM.at[q, w], rs.at[q, w], rv.at[q, w], xdev(1 if w == 0 else NX - 1)
        )

    def ry(q):
        return rc(FB.at[q - 2], YB.at[q], rys.at[q - 2], ryv.at[q - 2], ydev(q // 2))

    def step_a(q):
        yc(q).wait_recv()
        send_own(q)

    def step_b(q):
        xr(q).wait_recv()
        xt(q).start()
        pp(q, 1).start()
        xl(q).wait_recv()
        xg(q).start()
        pp(q, 2).start()

    def step_c(q):
        xt(q).wait_recv()
        xg(q).wait_recv()
        pp(q, 3).start()

    def step_d(q):
        j = q % 2
        for f in range(4):
            pp(q, f).wait_recv()
        pre_gate = lax.dot_general(RB[q, 0], WV[j, 0:FFL, :], nt, preferred_element_type=F32)
        pre_up = lax.dot_general(
            RB[q, 0], WV[j, FFL : 2 * FFL, :], nt, preferred_element_type=F32
        )
        hidden = lax.dot_general(
            RB[q, 1], WV[j, 2 * FFL : 3 * FFL, :], nt, preferred_element_type=F32
        )
        sg = jax.nn.sigmoid(pre_gate)
        act = pre_gate * sg
        prod = act * pre_up * hidden
        hi = prod.astype(BF)
        lo = (prod - hi.astype(F32)).astype(BF)
        ones = jnp.ones((8, FFL), BF)
        score = lax.dot_general(ones, hi, nt, preferred_element_type=F32)
        score = score + lax.dot_general(ones, lo, nt, preferred_element_type=F32)
        SC[q, :, 0:R] = score[0:1]
        gpg = (hidden * pre_up * sg * (1.0 + pre_gate * (1.0 - sg))).astype(BF)
        gpu = (hidden * act).astype(BF)
        for f in (4, 5, 6, 7, 3, 2, 1, 0):
            part = jnp.dot(gpg, WV[j, 0:FFL, f * FS : (f + 1) * FS], preferred_element_type=F32)
            part = part + jnp.dot(
                gpu, WV[j, FFL : 2 * FFL, f * FS : (f + 1) * FS], preferred_element_type=F32
            )
            PB[q, f] = part.astype(BF)
            if f == 7:
                px(q).start()

    def step_e(q):
        px(q).wait_recv()
        for f in (3, 2, 1, 0):
            PB[q, f] = (PB[q, f].astype(F32) + PX[q, f].astype(F32)).astype(BF)
            if f == 3:
                ra(q, 0).start()
                ra(q, 1).start()

    def step_f(q):
        for w in range(2):
            ra(q, w).wait_recv()
            lo, hi = w * (FS // 2), (w + 1) * (FS // 2)
            PB[q, 2 - w, :, lo:hi] = (
                PB[q, 2 - w, :, lo:hi].astype(F32) + RA[q, w].astype(F32)
            ).astype(BF)
            rm(q, w).start()

    def step_g(q):
        rm(q, 0).wait_recv()
        rm(q, 1).wait_recv()
        total = PB[q, 0].astype(F32) + RM[q, 0].astype(F32) + RM[q, 1].astype(F32)

        @pl.when(q < 2)
        def _():
            YB[q] = total.astype(BF)

        @pl.when(q >= 2)
        def _():
            FB[q - 2] = total.astype(BF)
            ry(q).start()

    def step_h(q):
        @pl.when(q >= 2)
        def _():
            ry(q).wait_recv()

        e = ((NY - q // 2) % NY) * 2 + q % 2
        for d in range(NZ):
            pick = PLB[e, :, d * TOK : (d + 1) * TOK].astype(F32)
            pick = pick * jnp.broadcast_to(WT[e, :, d * TOK : (d + 1) * TOK], (R, TOK))
            T[d] += lax.dot_general(pick.astype(BF), YB[q], tn, preferred_element_type=F32)

    def scx(k):
        return rc(SC, SCR.at[me_c], scs.at[k - 1], scv.at[k - 1], cdev(k))

    def scy(k):
        return rc(SCT, YSC.at[k - 1], sys_.at[k - 1], syv.at[k - 1], ydev(NY - k))

    def scz(k):
        return rc(SE.at[k], ZSC.at[NZ - k], szs.at[k - 1], szv.at[k - 1], zdev(k))

    @pl.loop(0, Q + 3)
    def _(i):
        pl.when(i < Q - 2)(lambda: step_a(i + 2))
        pl.when(i < Q)(lambda: step_b(i))
        pl.when((i >= 1) & (i < Q + 1))(lambda: step_e(i - 1))

        @pl.when(i < Q)
        def _():
            step_c(i)
            step_d(i)

        @pl.when(i == Q)
        def _():
            for k in range(1, NF):
                scx(k).start()

        pl.when((i >= 1) & (i < Q + 1))(lambda: step_f(i - 1))
        pl.when((i >= 2) & (i < Q + 2))(lambda: step_g(i - 2))
        pl.when((i >= 3) & (i < Q + 3))(lambda: step_h(i - 3))

    hf = FS // 2

    def zt(way, s):
        dev = zdev(1 if way == 0 else NZ - 1)
        if s == 1:
            lanes = pl.ds(way * hf, hf)
            src, dst = ZS.at[way, 0, :, lanes], ZR.at[way, 0, :, lanes]
        else:
            src, dst = ZS.at[way, s - 1], ZR.at[way, s - 1]
        return rc(src, dst, zrs.at[way, s - 1], zrv.at[way, s - 1], dev)

    for way in range(2):
        lanes = slice(way * hf, (way + 1) * hf)
        ZS[way, 0, :, lanes] = T[half, :, lanes].astype(BF)
        zt(way, 1).start()

    SCR[me_c] = SC[...]
    for k in range(1, NF):
        scx(k).wait_recv()
    total = SCR[0]
    for k in range(1, NF):
        total = total + SCR[k]
    SCT[...] = total
    for k in range(1, NY):
        scy(k).start()

    def ring(s):
        for way in range(2):
            zt(way, s - 1).wait_recv()
            d = half - (s - 1) if way == 0 else half + (s - 1)
            if s == 2:
                lanes = slice(way * hf, (way + 1) * hf)
                other = slice((1 - way) * hf, (2 - way) * hf)
                ZS[way, 1, :, lanes] = (
                    T[d, :, lanes] + ZR[way, 0, :, lanes].astype(F32)
                ).astype(BF)
                ZS[way, 1, :, other] = T[d, :, other].astype(BF)
            else:
                ZS[way, s - 1] = (T[d] + ZR[way, s - 2].astype(F32)).astype(BF)
            zt(way, s).start()

    ring(2)
    for dy in range(NY):
        if dy:
            scy(dy).wait_recv()
        for j in range(2):
            e = dy * 2 + j
            row = ((NY - dy) % NY) * 2 + j
            table = SCT[row, :, 0:R] if dy == 0 else YSC[dy - 1, row, :, 0:R]
            table = jnp.broadcast_to(table, (8, R))
            hi = table.astype(BF)
            lo = (table - hi.astype(F32)).astype(BF)
            spread = jnp.dot(hi, PLB[e], preferred_element_type=F32)
            spread = spread + jnp.dot(lo, PLB[e], preferred_element_type=F32)
            for d in range(NZ):
                SE[d, e : e + 1, :] = spread[0:1, d * TOK : (d + 1) * TOK]
    for k in range(1, NZ):
        scz(k).start()
    for s in range(3, half + 1):
        ring(s)

    gates = jnp.zeros((TOP, TOK), F32)
    ids = MB[0, 0:TOP, :]
    for d in range(NZ):
        if d:
            scz(NZ - d).wait_recv()
        piece = SE[0] if d == 0 else ZSC[d]
        for i in range(8):
            who = (2 * (((y + i // 2) % NY) * NZ + (z + d) % NZ) + i % 2).astype(F32)
            gates = gates + jnp.where(
                ids == who, jnp.broadcast_to(piece[i : i + 1, :], (TOP, TOK)), 0.0
            )
    gg[...] = gates

    for way in range(2):
        zt(way, half).wait_recv()
    out[...] = (
        T[0] + ZR[0, half - 1].astype(F32) + ZR[1, half - 1].astype(F32)
    ).astype(BF)

    for s in range(1, half + 1):
        for way in range(2):
            if s < half or way == 0:
                zm(way, s).wait_send()
            zx(way, s).wait_send()
            zt(way, s).wait_send()

    @pl.loop(0, Q)
    def _(q):
        for cp in (xr(q), xl(q), xt(q), xg(q), px(q), ra(q, 0), ra(q, 1), rm(q, 0), rm(q, 1)):
            cp.wait_send()
        for f in range(4):
            pp(q, f).wait_send()

    @pl.loop(2, Q)
    def _(q):
        yc(q).wait_send()
        ry(q).wait_send()

    for k in range(1, NF):
        scx(k).wait_send()
    for k in range(1, NY):
        scy(k).wait_send()
    for k in range(1, NZ):
        scz(k).wait_send()


def body(tokens, grad_out, expert_ids, gate_probs, gate_weight, up_weight, down_weight):
    meta = jnp.concatenate([expert_ids.astype(F32), gate_probs], axis=1).T
    V, S = pltpu.VMEM, pltpu.SemaphoreType.DMA
    scratch = [
        V((NZ, 2, TOK, FS), BF), V((NZ, 2 * TOP, TOK), F32),
        V((8, 1, NZ * TOK), F32), V((8, 1, NZ * TOK), F32), V((8, R, NZ * TOK), BF),
        V((Q - 2, 2, R, FS), BF), V((Q, 2, R, D), BF), V((2, 3 * FFL, D), BF),
        V((Q, NF, R, FS), BF), V((Q, 4, R, FS), BF), V((Q, 2, R, FS // 2), BF),
        V((Q, 2, R, FS), BF), V((Q - 2, R, FS), BF), V((Q, R, FS), BF),
        V((NZ, TOK, FS), F32), V((2, NZ // 2, TOK, FS), BF), V((2, NZ // 2, TOK, FS), BF),
        V((Q, 1, 256), F32), V((NF, Q, 1, 256), F32), V((Q, 1, 256), F32),
        V((NY - 1, Q, 1, 256), F32),
        V((NZ, 8, TOK), F32), V((NZ, 8, TOK), F32),
        S((3,)), S((2, NF, 3)),
        S((2, 4)), S((2, 4)), S((2, 4)), S((2, 4)), S((Q - 2,)), S((Q - 2,)),
        S((Q, 4)), S((Q, 4)), S((Q, 4)), S((Q, 4)), S((Q,)), S((Q,)),
        S((Q, 2)), S((Q, 2)), S((Q, 2)), S((Q, 2)), S((Q - 2,)), S((Q - 2,)), S((2, 4)), S((2, 4)),
        S((NF - 1,)), S((NF - 1,)), S((NY - 1,)), S((NY - 1,)), S((NZ - 1,)), S((NZ - 1,)),
    ]
    anyspec = pl.BlockSpec(memory_space=pl.ANY)
    vmem = pl.BlockSpec(memory_space=pltpu.VMEM)
    out, gates = pl.pallas_call(
        kernel,
        out_shape=(
            jax.ShapeDtypeStruct((TOK, FS), BF),
            jax.ShapeDtypeStruct((TOP, TOK), F32),
        ),
        in_specs=[anyspec] * 6,
        out_specs=(vmem, vmem),
        scratch_shapes=scratch,
        compiler_params=pltpu.CompilerParams(
            collective_id=0, has_side_effects=True, vmem_limit_bytes=60 * 1024 * 1024
        ),
        name="expert_grad",
    )(tokens, grad_out, meta, gate_weight, up_weight, down_weight)
    return out, gates.T.astype(BF)


def solution(mesh):
    in_specs = (
        P("expert", "ctx"),
        P("expert", "ctx"),
        P("expert", None),
        P("expert", None),
        P("expert", "ctx", None),
        P("expert", "ctx", None),
        P("expert", "ctx", None),
    )
    out_specs = (P("expert", "ctx"), P("expert", None))
    return jax.shard_map(body, mesh=mesh, in_specs=in_specs, out_specs=out_specs, check_vma=False)
```

time: 387 us -> 227 us (0.59)
  Pallas kernels: 0 us -> 220 us
  blocking collectives: 110 us -> 0 us
  waiting for transfers between devices: 99.8 us -> 0 us
  local copies, waits for them, and re-layouts: 56 us -> 1.57 us
  matrix products: 47.8 us -> 0 us
  other arithmetic: 36.1 us -> 3.24 us
  starting transfers between devices: 20.9 us -> 0 us
  between operations: 13.9 us -> 0.64 us
    pallas_call x0 -> x1, Pallas kernels: none -> 220 us  [body(): pl.pallas_call(kernel, out_shape=(jax.ShapeDtypeStruct((TOK, FS), BF), ja...]
    all_to_all x2 -> x0, blocking collectives: 85.4 us -> none  [the longest x1 46.2 us: body(): lax.all_to_all(sent_rows, 'expert', split_axis=0, concat_axis=0, tiled=True)]
    all_gather x2 -> x0, waiting for transfers between devices: 49.5 us -> none  [the longest x1 37.4 us: body(): lax.all_gather(got_grads, 'ctx', axis=2, tiled=True)]
    dot_general x7 -> x0, matrix products: 47.8 us -> none  [the longest x1 14.4 us: body(): jnp.einsum('secf,efd->secd', grad_pre_up, up_weight, preferred_element_ty...]
    another operation x3 -> x0, other arithmetic: 31 us -> none
    all_gather x2 -> x0, local copies, waits for them, and re-layouts: 25.8 us -> none  [the longest x1 13 us: body(): lax.all_gather(got_grads, 'ctx', axis=2, tiled=True)]
    all_to_all x2 -> x0, waiting for transfers between devices: 25.3 us -> none  [the longest x1 25.3 us: body(): lax.all_to_all(back_rows, 'expert', split_axis=0, concat_axis=0, tiled=True)]
    reduce_scatter x1 -> x0, waiting for transfers between devices: 25 us -> none  [body(): lax.psum_scatter(block_terms, 'ctx', scatter_dimension=3, tiled=True)]
  transfers between devices with their start and end apart: 5 -> 0, of which waited for: 4 -> 0; matrix products, arithmetic and copies ran while one was open for 11% -> 0% of each run, Pallas kernels for 0% -> 0%
where the time goes in v1:
time: 227 us; the launch traced here: 225 us
  Pallas kernels  220 us (97%)
  other arithmetic  3.24 us (1%)
    pallas_call x1, Pallas kernels, body(): pl.pallas_call(kernel, out_shape=(jax.ShapeDtypeStruct((TOK, FS), BF), ja...  220 us

profile of v1, /device:TPU:32, one launch (start us, length us, event | category | flops | bytes accessed | tf_op | source)
XLA Modules:
  0.0 225.0 jit_solution(12468097971538581172)
XLA Ops:
  0.6 0.7 convert_element_type.9
  1.3 1.3 maximum_bitcast_fusion.meta
  2.6 219.6 %expert_grad.1 = (bf16[128,512]{1,0:T(8,128)(2,1)}, f32[8,128]{1,0:T(8,128)}) custom-call(bf16[128,512]{1,0:T(8,128)(2,1)} %tok.1, bf16[128,512]{1,0:T(8,128)(2,1)} %grad.1, f32[16,128]{1,0:T(8,128)} %maximum_bitcast_fusion.meta, bf16[2,192,4096]{2,1,0:T(8,128)(2,1)} %wg.1, bf16[2,192,4096]{2,1,0:T(8,128)(2,1)} %wu.1, bf16[2,192,4096]{2,1,0:T(8,128)(2,1)} %wd.1), custom_call_target="tpu_custom_call" | custom-call | tf_op jit(solution)/shard_map/expert_grad/pallas_call | solution.py:465
  222.2 1.3 convert_bitcast_fusion
  223.5 1.6 copy.10

commit v2 on v1

--- a/solution.py
+++ b/solution.py
@@ -22,7 +22,7 @@
 
 
 def kernel(
-    tok, grad, meta, wg, wu, wd, out, gg,
+    tok, grad, ids_in, probs_in, wg, wu, wd, out, gg,
     XB, MB, KEY, WT, PLB, GB, RB, WV, PB, PX, RA, RM, FB, YB, T, ZS, ZR,
     SC, SCR, SCT, YSC, SE, ZSC,
     ls, ws, zs, zv, ms, mv, ys, yv, xs, xv, ps, pv, pxs, pxv, as_, av, rs, rv, rys, ryv, zrs, zrv,
@@ -49,10 +49,12 @@
     loads = [
         pltpu.make_async_copy(tok, XB.at[0, 0], ls.at[0]),
         pltpu.make_async_copy(grad, XB.at[0, 1], ls.at[1]),
-        pltpu.make_async_copy(meta, MB.at[0], ls.at[2]),
     ]
     for cp in loads:
         cp.start()
+
+    MB[0, 0:TOP, :] = ids_in[...].astype(F32)
+    MB[0, TOP : 2 * TOP, :] = probs_in[...]
 
     barrier = pltpu.get_barrier_semaphore()
     peers = [cdev(k) for k in range(1, NF)] + [ydev(k) for k in range(1, NY)]
@@ -63,14 +65,12 @@
     for cp in loads:
         cp.wait()
 
-    def zx(way, s):
+    def zx(way, s, a):
         if way == 0:
-            si, di, dev, part = (NZ - (s - 1)) % NZ, NZ - s, zdev(1), 0
+            si, di, dev = (NZ - (s - 1)) % NZ, NZ - s, zdev(1)
         else:
-            si, di, dev, part = s - 1, s, zdev(NZ - 1), 1
-        if s < NZ // 2:
-            return rc(XB.at[si], XB.at[di], zs.at[way, s - 1], zv.at[way, s - 1], dev)
-        return rc(XB.at[si, part], XB.at[di, part], zs.at[way, s - 1], zv.at[way, s - 1], dev)
+            si, di, dev = s - 1, s, zdev(NZ - 1)
+        return rc(XB.at[si, a], XB.at[di, a], zs.at[way, s - 1, a], zv.at[way, s - 1, a], dev)
 
     def zm(way, s):
         if way == 0:
@@ -103,7 +103,9 @@
     half = NZ // 2
     for way in range(2):
         zm(way, 1).start()
-        zx(way, 1).start()
+    for a in range(2):
+        for way in range(2):
+            zx(way, 1, a).start()
 
     def wload(j, f, m):
         xo = (0, NX - 1, 1, 2)[f % 4]
@@ -123,9 +125,12 @@
                 zm(way, s).wait_recv()
                 if s + 1 < half or (s + 1 == half and way == 0):
                     zm(way, s + 1).start()
-            zx(way, s).wait_recv()
-            if s < half:
-                zx(way, s + 1).start()
+        for a in range(2):
+            for way in range(2):
+                if s < half or a == way:
+                    zx(way, s, a).wait_recv()
+                if s + 1 < half or (s + 1 == half and a == way):
+                    zx(way, s + 1, a).start()
         key(NZ - s)
         if s < half:
             key(s)
@@ -314,25 +319,25 @@
     def scz(k):
         return rc(SE.at[k], ZSC.at[NZ - k], szs.at[k - 1], szv.at[k - 1], zdev(k))
 
-    @pl.loop(0, Q + 3)
-    def _(i):
-        pl.when(i < Q - 2)(lambda: step_a(i + 2))
-        pl.when(i < Q)(lambda: step_b(i))
-        pl.when((i >= 1) & (i < Q + 1))(lambda: step_e(i - 1))
-
-        @pl.when(i < Q)
-        def _():
-            step_c(i)
-            step_d(i)
-
-        @pl.when(i == Q)
+    def during(q, run):
+        pl.when((q >= 0) & (q < Q))(lambda: run(q))
+
+    @pl.loop(0, Q + 5)
+    def _(t):
+        pl.when((t >= 1) & (t < Q - 1))(lambda: step_a(t + 1))
+        during(t, step_b)
+        during(t - 2, step_e)
+        during(t - 1, step_c)
+        during(t - 1, step_d)
+
+        @pl.when(t == Q)
         def _():
             for k in range(1, NF):
                 scx(k).start()
 
-        pl.when((i >= 1) & (i < Q + 1))(lambda: step_f(i - 1))
-        pl.when((i >= 2) & (i < Q + 2))(lambda: step_g(i - 2))
-        pl.when((i >= 3) & (i < Q + 3))(lambda: step_h(i - 3))
+        during(t - 3, step_f)
+        during(t - 4, step_g)
+        during(t - 5, step_h)
 
     hf = FS // 2
 
@@ -406,7 +411,7 @@
             gates = gates + jnp.where(
                 ids == who, jnp.broadcast_to(piece[i : i + 1, :], (TOP, TOK)), 0.0
             )
-    gg[...] = gates
+    gg[...] = gates.astype(BF)
 
     for way in range(2):
         zt(way, half).wait_recv()
@@ -418,7 +423,9 @@
         for way in range(2):
             if s < half or way == 0:
                 zm(way, s).wait_send()
-            zx(way, s).wait_send()
+            for a in range(2):
+                if s < half or a == way:
+                    zx(way, s, a).wait_send()
             zt(way, s).wait_send()
 
     @pl.loop(0, Q)
@@ -442,7 +449,6 @@
 
 
 def body(tokens, grad_out, expert_ids, gate_probs, gate_weight, up_weight, down_weight):
-    meta = jnp.concatenate([expert_ids.astype(F32), gate_probs], axis=1).T
     V, S = pltpu.VMEM, pltpu.SemaphoreType.DMA
     scratch = [
         V((NZ, 2, TOK, FS), BF), V((NZ, 2 * TOP, TOK), F32),
@@ -454,8 +460,8 @@
         V((Q, 1, 256), F32), V((NF, Q, 1, 256), F32), V((Q, 1, 256), F32),
         V((NY - 1, Q, 1, 256), F32),
         V((NZ, 8, TOK), F32), V((NZ, 8, TOK), F32),
-        S((3,)), S((2, NF, 3)),
-        S((2, 4)), S((2, 4)), S((2, 4)), S((2, 4)), S((Q - 2,)), S((Q - 2,)),
+        S((2,)), S((2, NF, 3)),
+        S((2, 4, 2)), S((2, 4, 2)), S((2, 4)), S((2, 4)), S((Q - 2,)), S((Q - 2,)),
         S((Q, 4)), S((Q, 4)), S((Q, 4)), S((Q, 4)), S((Q,)), S((Q,)),
         S((Q, 2)), S((Q, 2)), S((Q, 2)), S((Q, 2)), S((Q - 2,)), S((Q - 2,)), S((2, 4)), S((2, 4)),
         S((NF - 1,)), S((NF - 1,)), S((NY - 1,)), S((NY - 1,)), S((NZ - 1,)), S((NZ - 1,)),
@@ -466,17 +472,17 @@
         kernel,
         out_shape=(
             jax.ShapeDtypeStruct((TOK, FS), BF),
-            jax.ShapeDtypeStruct((TOP, TOK), F32),
+            jax.ShapeDtypeStruct((TOP, TOK), BF),
         ),
-        in_specs=[anyspec] * 6,
+        in_specs=[anyspec] * 2 + [vmem] * 2 + [anyspec] * 3,
         out_specs=(vmem, vmem),
         scratch_shapes=scratch,
         compiler_params=pltpu.CompilerParams(
             collective_id=0, has_side_effects=True, vmem_limit_bytes=60 * 1024 * 1024
         ),
         name="expert_grad",
-    )(tokens, grad_out, meta, gate_weight, up_weight, down_weight)
-    return out, gates.T.astype(BF)
+    )(tokens, grad_out, expert_ids.T, gate_probs.T, gate_weight, up_weight, down_weight)
+    return out, gates.T
 
 
 def solution(mesh):

time: 227 us -> 182 us (0.80)
  Pallas kernels: 220 us -> 178 us
  other arithmetic: 3.24 us -> 0 us
    pallas_call x1, Pallas kernels: 220 us -> 178 us  [body(): pl.pallas_call(kernel, out_shape=(jax.ShapeDtypeStruct((TOK, FS), BF), ja...]
where the time goes in v2:
time: 182 us; the launch traced here: 181 us
  Pallas kernels  178 us (98%)
  local copies, waits for them, and re-layouts  2.83 us (2%)
    pallas_call x1, Pallas kernels, body(): pl.pallas_call(kernel, out_shape=(jax.ShapeDtypeStruct((TOK, FS), BF), ja...  178 us

profile of v2, /device:TPU:32, one launch (start us, length us, event | category | flops | bytes accessed | tf_op | source)
XLA Modules:
  0.0 181.3 jit_solution(4051453844750197581)
XLA Ops:
  0.6 177.8 %expert_grad.1 = (bf16[128,512]{1,0:T(8,128)(2,1)}, bf16[8,128]{1,0:T(8,128)(2,1)}) custom-call(bf16[128,512]{1,0:T(8,128)(2,1)} %tok.1, bf16[128,512]{1,0:T(8,128)(2,1)} %grad.1, s32[8,128]{1,0:T(8,128)} %bitcast.3, f32[8,128]{1,0:T(8,128)} %bitcast.4, bf16[2,192,4096]{2,1,0:T(8,128)(2,1)} %wg.1, bf16[2,192,4096]{2,1,0:T(8,128)(2,1)} %wu.1, ...), custom_call_target="tpu_custom_call" | custom-call | tf_op jit(solution)/shard_map/expert_grad/pallas_call | solution.py:471
  178.5 1.6 copy.11
  180.0 1.3 copy.12

commit v3 on v2

--- a/solution.py
+++ b/solution.py
@@ -23,9 +23,9 @@
 
 def kernel(
     tok, grad, ids_in, probs_in, wg, wu, wd, out, gg,
-    XB, MB, KEY, WT, PLB, GB, RB, WV, PB, PX, RA, RM, FB, YB, T, ZS, ZR,
+    XB, XA, MB, KEY, WT, PLB, GB, GA, RB, WV, PB, PX, RA, RM, FB, YB, T, ZS, ZR,
     SC, SCR, SCT, YSC, SE, ZSC,
-    ls, ws, zs, zv, ms, mv, ys, yv, xs, xv, ps, pv, pxs, pxv, as_, av, rs, rv, rys, ryv, zrs, zrv,
+    ls, ws, zs, zv, zas, zav, xas, xav, ms, mv, ys, yv, yas, yav, xs, xv, ps, pv, pxs, pxv, as_, av, rs, rv, rys, ryv, zrs, zrv,
     scs, scv, sys_, syv, szs, szv,
 ):
     me_e, me_c = lax.axis_index("expert"), lax.axis_index("ctx")
@@ -71,6 +71,16 @@
         else:
             si, di, dev = s - 1, s, zdev(NZ - 1)
         return rc(XB.at[si, a], XB.at[di, a], zs.at[way, s - 1, a], zv.at[way, s - 1, a], dev)
+
+    def za(way, s, a):
+        if way == 0:
+            si, di, dev = (NZ - (s - 1)) % NZ, NZ - s, zdev(1)
+        else:
+            si, di, dev = s - 1, s, zdev(NZ - 1)
+        return rc(XA.at[si, a], XA.at[di, a], zas.at[way, s - 1, a], zav.at[way, s - 1, a], dev)
+
+    def xa(a):
+        return rc(XB.at[0, a], XA.at[0, a], xas.at[a], xav.at[a], xdev(2))
 
     def zm(way, s):
         if way == 0:
@@ -106,6 +116,8 @@
     for a in range(2):
         for way in range(2):
             zx(way, 1, a).start()
+    for a in range(2):
+        xa(a).start()
 
     def wload(j, f, m):
         xo = (0, NX - 1, 1, 2)[f % 4]
@@ -131,6 +143,11 @@
                     zx(way, s, a).wait_recv()
                 if s + 1 < half or (s + 1 == half and a == way):
                     zx(way, s + 1, a).start()
+        if s == half - 1:
+            for a in range(2):
+                xa(a).wait_recv()
+                for way in range(2):
+                    za(way, 1, a).start()
         key(NZ - s)
         if s < half:
             key(s)
@@ -141,8 +158,8 @@
         hit = jnp.broadcast_to(KEY[e], (R, NZ * TOK)) == rowid
         PLB[e] = jnp.where(hit, 1.0, 0.0).astype(BF)
 
-    def gather(e, a):
-        slab = XB[:, a].reshape(NZ * TOK, FS)
+    def gather(e, a, slabs):
+        slab = slabs[:, a].reshape(NZ * TOK, FS)
         return jnp.dot(PLB[e], slab, preferred_element_type=F32).astype(BF)
 
     def own(q):
@@ -157,23 +174,14 @@
     def xl(q):
         return rc(own(q), fsl(q, 2), xs.at[q, 1], xv.at[q, 1], xdev(NX - 1))
 
-    def xt(q):
-        return rc(
-            RB.at[q, 0, :, pl.ds(FS, FS)], RB.at[q, 0, :, pl.ds(3 * FS, FS)],
-            xs.at[q, 2], xv.at[q, 2], xdev(1),
-        )
-
-    def xg(q):
-        return rc(
-            RB.at[q, 1, :, pl.ds(2 * FS, FS)], RB.at[q, 1, :, pl.ds(3 * FS, FS)],
-            xs.at[q, 3], xv.at[q, 3], xdev(NX - 1),
-        )
-
     def pp(q, f):
         return rc(fsl(q, f), fsl(q, 4 + f), ps.at[q, f], pv.at[q, f], partner)
 
     def yc(q):
         return rc(GB.at[q - 2], own(q), ys.at[q - 2], yv.at[q - 2], ydev(NY - q // 2))
+
+    def ya(q):
+        return rc(GA.at[q - 2], fsl(q, 3), yas.at[q - 2], yav.at[q - 2], ydev(NY - q // 2))
 
     def send_own(q):
         xr(q).start()
@@ -184,7 +192,7 @@
     def _(q):
         place(q)
         for a in range(2):
-            RB[q, a, :, 0:FS] = gather(q, a)
+            RB[q, a, :, 0:FS] = gather(q, a, XB)
         send_own(q)
 
     @pl.loop(2, Q)
@@ -192,7 +200,7 @@
         e = ((NY - q // 2) % NY) * 2 + q % 2
         place(e)
         for a in range(2):
-            GB[q - 2, a] = gather(e, a)
+            GB[q - 2, a] = gather(e, a, XB)
         yc(q).start()
 
     for cp in wloads:
@@ -204,7 +212,7 @@
     tn = (((0,), (0,)), ((), ()))
 
     def px(q):
-        return rc(PB.at[q, pl.ds(4, 4)], PX.at[q], pxs.at[q], pxv.at[q], partner)
+        return rc(PB.at[q, pl.ds(4, 4)], PX.at[q % 4], pxs.at[q], pxv.at[q], partner)
 
     def ra(q, w):
         return rc(
@@ -226,15 +234,12 @@
 
     def step_b(q):
         xr(q).wait_recv()
-        xt(q).start()
         pp(q, 1).start()
         xl(q).wait_recv()
-        xg(q).start()
         pp(q, 2).start()
 
     def step_c(q):
-        xt(q).wait_recv()
-        xg(q).wait_recv()
+        ya(q).wait_recv()
         pp(q, 3).start()
 
     def step_d(q):
@@ -271,7 +276,7 @@
     def step_e(q):
         px(q).wait_recv()
         for f in (3, 2, 1, 0):
-            PB[q, f] = (PB[q, f].astype(F32) + PX[q, f].astype(F32)).astype(BF)
+            PB[q, f] = (PB[q, f].astype(F32) + PX[q % 4, f].astype(F32)).astype(BF)
             if f == 3:
                 ra(q, 0).start()
                 ra(q, 1).start()
@@ -322,22 +327,53 @@
     def during(q, run):
         pl.when((q >= 0) & (q < Q))(lambda: run(q))
 
-    @pl.loop(0, Q + 5)
+    def ring_a(s):
+        for a in range(2):
+            for way in range(2):
+                if s < half or a == way:
+                    za(way, s, a).wait_recv()
+                if s + 1 < half or (s + 1 == half and a == way):
+                    za(way, s + 1, a).start()
+
+    ring_a(1)
+    step_b(0)
+    step_a(2)
+    ring_a(2)
+    step_b(1)
+    step_a(3)
+    ring_a(3)
+    step_a(4)
+    ring_a(4)
+
+    @pl.loop(0, 2)
+    def _(q):
+        for a in range(2):
+            RB[q, a, :, 3 * FS : 4 * FS] = gather(q, a, XA)
+        pp(q, 3).start()
+
+    @pl.loop(2, Q)
+    def _(q):
+        e = ((NY - q // 2) % NY) * 2 + q % 2
+        for a in range(2):
+            GA[q - 2, a] = gather(e, a, XA)
+        ya(q).start()
+
+    @pl.loop(0, Q + 4)
     def _(t):
-        pl.when((t >= 1) & (t < Q - 1))(lambda: step_a(t + 1))
-        during(t, step_b)
-        during(t - 2, step_e)
-        during(t - 1, step_c)
-        during(t - 1, step_d)
-
-        @pl.when(t == Q)
+        pl.when(t < Q - 5)(lambda: step_a(t + 5))
+        pl.when(t < Q - 2)(lambda: step_b(t + 2))
+        pl.when((t >= 1) & (t < Q - 1))(lambda: step_c(t + 1))
+        during(t - 1, step_e)
+        during(t, step_d)
+
+        @pl.when(t == Q - 1)
         def _():
             for k in range(1, NF):
                 scx(k).start()
 
-        during(t - 3, step_f)
-        during(t - 4, step_g)
-        during(t - 5, step_h)
+        during(t - 2, step_f)
+        during(t - 3, step_g)
+        during(t - 4, step_h)
 
     hf = FS // 2
 
@@ -419,6 +455,8 @@
         T[0] + ZR[0, half - 1].astype(F32) + ZR[1, half - 1].astype(F32)
     ).astype(BF)
 
+    for a in range(2):
+        xa(a).wait_send()
     for s in range(1, half + 1):
         for way in range(2):
             if s < half or way == 0:
@@ -426,11 +464,12 @@
             for a in range(2):
                 if s < half or a == way:
                     zx(way, s, a).wait_send()
+                    za(way, s, a).wait_send()
             zt(way, s).wait_send()
 
     @pl.loop(0, Q)
     def _(q):
-        for cp in (xr(q), xl(q), xt(q), xg(q), px(q), ra(q, 0), ra(q, 1), rm(q, 0), rm(q, 1)):
+        for cp in (xr(q), xl(q), px(q), ra(q, 0), ra(q, 1), rm(q, 0), rm(q, 1)):
             cp.wait_send()
         for f in range(4):
             pp(q, f).wait_send()
@@ -438,6 +477,7 @@
     @pl.loop(2, Q)
     def _(q):
         yc(q).wait_send()
+        ya(q).wait_send()
         ry(q).wait_send()
 
     for k in range(1, NF):
@@ -451,18 +491,19 @@
 def body(tokens, grad_out, expert_ids, gate_probs, gate_weight, up_weight, down_weight):
     V, S = pltpu.VMEM, pltpu.SemaphoreType.DMA
     scratch = [
-        V((NZ, 2, TOK, FS), BF), V((NZ, 2 * TOP, TOK), F32),
+        V((NZ, 2, TOK, FS), BF), V((NZ, 2, TOK, FS), BF), V((NZ, 2 * TOP, TOK), F32),
         V((8, 1, NZ * TOK), F32), V((8, 1, NZ * TOK), F32), V((8, R, NZ * TOK), BF),
-        V((Q - 2, 2, R, FS), BF), V((Q, 2, R, D), BF), V((2, 3 * FFL, D), BF),
-        V((Q, NF, R, FS), BF), V((Q, 4, R, FS), BF), V((Q, 2, R, FS // 2), BF),
+        V((Q - 2, 2, R, FS), BF), V((Q - 2, 2, R, FS), BF), V((Q, 2, R, D), BF), V((2, 3 * FFL, D), BF),
+        V((Q, NF, R, FS), BF), V((4, 4, R, FS), BF), V((Q, 2, R, FS // 2), BF),
         V((Q, 2, R, FS), BF), V((Q - 2, R, FS), BF), V((Q, R, FS), BF),
         V((NZ, TOK, FS), F32), V((2, NZ // 2, TOK, FS), BF), V((2, NZ // 2, TOK, FS), BF),
         V((Q, 1, 256), F32), V((NF, Q, 1, 256), F32), V((Q, 1, 256), F32),
         V((NY - 1, Q, 1, 256), F32),
         V((NZ, 8, TOK), F32), V((NZ, 8, TOK), F32),
         S((2,)), S((2, NF, 3)),
-        S((2, 4, 2)), S((2, 4, 2)), S((2, 4)), S((2, 4)), S((Q - 2,)), S((Q - 2,)),
-        S((Q, 4)), S((Q, 4)), S((Q, 4)), S((Q, 4)), S((Q,)), S((Q,)),
+        S((2, 4, 2)), S((2, 4, 2)), S((2, 4, 2)), S((2, 4, 2)), S((2,)), S((2,)),
+        S((2, 4)), S((2, 4)), S((Q - 2,)), S((Q - 2,)), S((Q - 2,)), S((Q - 2,)),
+        S((Q, 2)), S((Q, 2)), S((Q, 4)), S((Q, 4)), S((Q,)), S((Q,)),
         S((Q, 2)), S((Q, 2)), S((Q, 2)), S((Q, 2)), S((Q - 2,)), S((Q - 2,)), S((2, 4)), S((2, 4)),
         S((NF - 1,)), S((NF - 1,)), S((NY - 1,)), S((NY - 1,)), S((NZ - 1,)), S((NZ - 1,)),
     ]

time: 182 us -> 160 us (0.88)
  Pallas kernels: 178 us -> 156 us
    pallas_call x1, Pallas kernels: 178 us -> 156 us  [body(): pl.pallas_call(kernel, out_shape=(jax.ShapeDtypeStruct((TOK, FS), BF), ja...]
where the time goes in v3:
time: 160 us; the launch traced here: 159 us
  Pallas kernels  156 us (98%)
  local copies, waits for them, and re-layouts  2.83 us (2%)
    pallas_call x1, Pallas kernels, body(): pl.pallas_call(kernel, out_shape=(jax.ShapeDtypeStruct((TOK, FS), BF), ja...  156 us

profile of v3, /device:TPU:32, one launch (start us, length us, event | category | flops | bytes accessed | tf_op | source)
XLA Modules:
  0.0 159.4 jit_solution(13325302608430809642)
XLA Ops:
  0.6 156.0 %expert_grad.1 = (bf16[128,512]{1,0:T(8,128)(2,1)}, bf16[8,128]{1,0:T(8,128)(2,1)}) custom-call(bf16[128,512]{1,0:T(8,128)(2,1)} %tok.1, bf16[128,512]{1,0:T(8,128)(2,1)} %grad.1, s32[8,128]{1,0:T(8,128)} %bitcast.3, f32[8,128]{1,0:T(8,128)} %bitcast.4, bf16[2,192,4096]{2,1,0:T(8,128)(2,1)} %wg.1, bf16[2,192,4096]{2,1,0:T(8,128)(2,1)} %wu.1, ...), custom_call_target="tpu_custom_call" | custom-call | tf_op jit(solution)/shard_map/expert_grad/pallas_call | solution.py:512
  156.6 1.6 copy.11
  158.2 1.3 copy.12

commit v4 on v3

v4 whole, which is shorter than its diff:
```python
import jax
import jax.numpy as jnp
from jax import lax
from jax.experimental import pallas as pl
from jax.experimental.pallas import tpu as pltpu
from jax.sharding import PartitionSpec as P

MESH = pl.DeviceIdType.MESH
NY, NZ, NX = 4, 8, 4
CAP, TOK, TOP = 18, 128, 8
R = NZ * CAP
FS, FFL, NF = 512, 192, 8
D = FS * NF
Q = NY
U = 2 * NY - 1
BF, F32 = jnp.bfloat16, jnp.float32
POS = (0, 1, 3, 5, 7, 6, 4, 2)
NEAR = ((0, 48, 0, 3), (48, 32, 2, 5), (80, 64, 4, 8))
FAR = ((0, 80, 0, 5), (80, 64, 4, 8))


def rc(src, dst, ss, rs, dev):
    return pltpu.make_async_remote_copy(
        src_ref=src, dst_ref=dst, send_sem=ss, recv_sem=rs, device_id=dev, device_id_type=MESH
    )


def kernel(
    tok, grad, ids_in, probs_in, wg, wu, wd, out, gg,
    XB, XA, MB, KEY, WT, PLB, GB, GA, RB, WV, PB, RM, FB, YB, YF, T, TF, ZS, ZR, ZSF, ZRF, OS, OR,
    SC, SCR, SCT, YSC, SE, ZSC,
    ls, ws, wrs, wrv, zs, zv, zas, zav, xas, xav, ms, mv, ys, yv, yas, yav, xs, xv,
    fys, fyv, rs, rv, rys, ryv, zrs, zrv, fzs, fzv, os_, ov, scs, scv, sys_, syv, szs, szv,
):
    me_e, me_c = lax.axis_index("expert"), lax.axis_index("ctx")
    y, z = me_e // NZ, me_e % NZ
    x, c = me_c // 2, me_c % 2

    def xdev(dx):
        return {"ctx": ((x + dx) % NX) * 2 + c}

    partner = {"ctx": x * 2 + 1 - c}

    def ydev(dy):
        return {"expert": ((y + dy) % NY) * NZ + z}

    def zdev(dz):
        return {"expert": y * NZ + (z + dz) % NZ}

    def cdev(k):
        return {"ctx": (me_c + k) % NF}

    loads = [
        pltpu.make_async_copy(tok, XB.at[0, 0], ls.at[0]),
        pltpu.make_async_copy(grad, XB.at[0, 1], ls.at[1]),
    ]
    for cp in loads:
        cp.start()

    MB[0, 0:TOP, :] = ids_in[...].astype(F32)
    MB[0, TOP : 2 * TOP, :] = probs_in[...]

    barrier = pltpu.get_barrier_semaphore()
    peers = [cdev(k) for k in range(1, NF)] + [ydev(k) for k in range(1, NY)]
    peers += [zdev(k) for k in range(1, NZ)]
    peers += [{**ydev(k), **partner} for k in range(1, NY)]
    for peer in peers:
        pl.semaphore_signal(barrier, inc=1, device_id=peer, device_id_type=MESH)
    pl.semaphore_wait(barrier, len(peers))
    for cp in loads:
        cp.wait()

    def zx(way, s, a):
        if way == 0:
            si, di, dev = (NZ - (s - 1)) % NZ, NZ - s, zdev(1)
        else:
            si, di, dev = s - 1, s, zdev(NZ - 1)
        si, di = POS[si], POS[di]
        return rc(XB.at[si, a], XB.at[di, a], zs.at[way, s - 1, a], zv.at[way, s - 1, a], dev)

    def za(way, s, a):
        if way == 0:
            si, di, dev = (NZ - (s - 1)) % NZ, NZ - s, zdev(1)
        else:
            si, di, dev = s - 1, s, zdev(NZ - 1)
        si, di = POS[si], POS[di]
        return rc(XA.at[si, a], XA.at[di, a], zas.at[way, s - 1, a], zav.at[way, s - 1, a], dev)

    def xa(a):
        return rc(XB.at[0, a], XA.at[0, a], xas.at[a], xav.at[a], xdev(2))

    def zm(way, s):
        if way == 0:
            si, di, dev = (NZ - (s - 1)) % NZ, NZ - s, zdev(1)
        else:
            si, di, dev = s - 1, s, zdev(NZ - 1)
        return rc(MB.at[si], MB.at[di], ms.at[way, s - 1], mv.at[way, s - 1], dev)

    lane = lax.broadcasted_iota(jnp.int32, (TOK, TOK), 1)
    sub = lax.broadcasted_iota(jnp.int32, (TOK, TOK), 0)
    before = (sub < lane).astype(BF)
    erow = lax.broadcasted_iota(jnp.int32, (8, TOK), 0)
    dyrow = erow // 2
    expert = (2 * (((y + dyrow) % NY) * NZ + z) + (erow - 2 * dyrow)).astype(F32)

    def key(d):
        member = jnp.zeros((8, TOK), F32)
        weight = jnp.zeros((8, TOK), F32)
        for k in range(TOP):
            hit = jnp.broadcast_to(MB[d, k : k + 1, :], (8, TOK)) == expert
            member = member + jnp.where(hit, 1.0, 0.0)
            prob = jnp.broadcast_to(MB[d, TOP + k : TOP + k + 1, :], (8, TOK))
            weight = weight + jnp.where(hit, prob, 0.0)
        rank = jnp.dot(member.astype(BF), before, preferred_element_type=F32)
        p = POS[d]
        slot = jnp.where(member > 0.5, rank + float(p * CAP), -1.0)
        for e in range(8):
            KEY[e, :, p * TOK : (p + 1) * TOK] = slot[e : e + 1]
            WT[e, :, p * TOK : (p + 1) * TOK] = weight[e : e + 1]

    half = NZ // 2
    for way in range(2):
        zm(way, 1).start()
    for a in range(2):
        for way in range(2):
            zx(way, 1, a).start()
    for a in range(2):
        xa(a).start()

    def wslice(m, f, expert_of):
        xo = (0, NX - 1, 1, 2)[f // 2]
        ctx = ((x + xo) % NX) * 2 + f % 2
        src = (wg, wu, wd)[m].at[expert_of, :, pl.ds(pl.multiple_of(ctx * FS, FS), FS)]
        rows = pl.ds(pl.multiple_of(c * FFL, FFL), FFL)
        return src, WV.at[m, rows, pl.ds(f * FS, FS)]

    def wload(m, f):
        return pltpu.make_async_copy(*wslice(m, f, c), ws.at[m, f])

    def wgive(m, f):
        return rc(*wslice(m, f, 1 - c), wrs.at[m, f], wrv.at[m, f], partner)

    for m in range(3):
        for f in range(NF):
            wgive(m, f).start()
            wload(m, f).start()

    @pl.loop(0, 8)
    def _(e):
        PLB[e] = jnp.zeros((R, NZ * TOK), BF)

    def place(e, part):
        r0, n, p0, p1 = part
        rowid = lax.broadcasted_iota(jnp.int32, (n, (p1 - p0) * TOK), 0).astype(F32) + float(r0)
        keys = jnp.broadcast_to(KEY[e, :, p0 * TOK : p1 * TOK], (n, (p1 - p0) * TOK))
        PLB[e, r0 : r0 + n, p0 * TOK : p1 * TOK] = jnp.where(keys == rowid, 1.0, 0.0).astype(BF)

    def gather(e, a, slabs, part):
        r0, n, p0, p1 = part
        slab = slabs[p0:p1, a].reshape((p1 - p0) * TOK, FS)
        pick = PLB[e, r0 : r0 + n, p0 * TOK : p1 * TOK]
        return jnp.dot(pick, slab, preferred_element_type=F32).astype(BF)

    def fsl(q, f, part):
        lanes = pl.ds(pl.multiple_of(f * FS, FS), FS)
        return RB.at[q, :, pl.ds(part[0], part[1]), lanes]

    def pair(u):
        return (u + 1) // 2, (u + 1) % 2

    def ydst(u):
        q, j = pair(u)
        return {"expert": ((y + NY - q) % NY) * NZ + z, "ctx": x * 2 + j}

    def rows(buf, u, part):
        return buf.at[u, :, pl.ds(part[0], part[1])]

    def yc(u, k):
        return rc(
            rows(GB, u, NEAR[k]), fsl(pair(u)[0], c, NEAR[k]),
            ys.at[k, u], yv.at[k, pair(u)[0], c], ydst(u),
        )

    def ya(u, k):
        return rc(
            rows(GA, u, FAR[k]), fsl(pair(u)[0], 6 + c, FAR[k]),
            yas.at[k, u], yav.at[k, pair(u)[0], c], ydst(u),
        )

    def pc(k):
        return rc(rows(GB, 0, NEAR[k]), fsl(0, c, NEAR[k]), ys.at[k, 0], yv.at[k, 0, c], partner)

    def pa(k):
        return rc(rows(GA, 0, FAR[k]), fsl(0, 6 + c, FAR[k]), yas.at[k, 0], yav.at[k, 0, c], partner)

    def got(q, cs, k):
        part = NEAR[k]
        return rc(rows(GB, 0, part), fsl(q, cs, part), ys.at[k, 0], yv.at[k, q, cs], partner)

    def got_a(q, cs, k):
        part = FAR[k]
        return rc(rows(GA, 0, part), fsl(q, 6 + cs, part), yas.at[k, 0], yav.at[k, q, cs], partner)

    def xw(q, cs, w, k):
        dev = xdev(1 if w == 0 else NX - 1)
        return rc(
            fsl(q, cs, NEAR[k]), fsl(q, 2 + 2 * w + cs, NEAR[k]),
            xs.at[k, q, w, cs], xv.at[k, q, w, cs], dev,
        )

    def send_x(q, cs, k):
        xw(q, cs, 0, k).start()
        xw(q, cs, 1, k).start()

    def step_a(k):
        @pl.loop(1, Q)
        def _(q):
            for cs in range(2):
                got(q, cs, k).wait_recv()
                send_x(q, cs, k)

    lanes_own = pl.ds(pl.multiple_of(c * FS, FS), FS)
    lanes_far = pl.ds(pl.multiple_of((6 + c) * FS, FS), FS)

    def near(k):
        part = NEAR[k]
        r0, r1 = part[0], part[0] + part[1]
        place(c, part)
        for a in range(2):
            RB[0, a, r0:r1, lanes_own] = gather(c, a, XB, part)
        send_x(0, c, k)
        place(1 - c, part)
        for a in range(2):
            GB[0, a, r0:r1] = gather(1 - c, a, XB, part)
        pc(k).start()

        @pl.loop(1, U)
        def _(u):
            q, j = pair(u)
            e = ((NY - q) % NY) * 2 + j
            place(e, part)
            for a in range(2):
                GB[u, a, r0:r1] = gather(e, a, XB, part)
            yc(u, k).start()

        got(0, 1 - c, k).wait_recv()
        send_x(0, 1 - c, k)

    def far(k):
        part = FAR[k]
        r0, r1 = part[0], part[0] + part[1]

        @pl.loop(1, U)
        def _(u):
            q, j = pair(u)
            e = ((NY - q) % NY) * 2 + j
            for a in range(2):
                GA[u, a, r0:r1] = gather(e, a, XA, part)
            ya(u, k).start()

        for a in range(2):
            GA[0, a, r0:r1] = gather(1 - c, a, XA, part)
        pa(k).start()
        for a in range(2):
            RB[0, a, r0:r1, lanes_far] = gather(c, a, XA, part)

    def ring_a(s):
        for a in range(2):
            for way in range(2):
                if s < half or a == way:
                    za(way, s, a).wait_recv()
                if s + 1 < half or (s + 1 == half and a == way):
                    za(way, s + 1, a).start()

    key(0)
    for d in range(NZ):
        T[d] = jnp.zeros((TOK, FS), F32)
        TF[d] = jnp.zeros((TOK, FS), F32)
    for s in range(1, half + 1):
        for way in range(2):
            if s < half or way == 0:
                zm(way, s).wait_recv()
                if s + 1 < half or (s + 1 == half and way == 0):
                    zm(way, s + 1).start()
        key(NZ - s)
        if s < half:
            key(s)
        for a in range(2):
            for way in range(2):
                if s < half or a == way:
                    zx(way, s, a).wait_recv()
                if s + 1 < half or (s + 1 == half and a == way):
                    zx(way, s + 1, a).start()
        if s == 1:
            near(0)
        elif s == 2:
            near(1)
        elif s == half - 1:
            for a in range(2):
                xa(a).wait_recv()
                for way in range(2):
                    za(way, 1, a).start()
            step_a(0)
        else:
            near(2)
    step_a(1)
    ring_a(1)
    ring_a(2)
    far(0)
    step_a(2)
    ring_a(3)
    ring_a(4)
    far(1)
    for m in range(3):
        for f in range(NF):
            wload(m, f).wait()
            wgive(m, f).wait_recv()

    nt = (((1,), (1,)), ((), ()))
    tn = (((0,), (0,)), ((), ()))

    def rm(q, w, cs):
        return rc(
            PB.at[q, 4 - 2 * w + cs], RM.at[q, w, cs], rs.at[q, w, cs], rv.at[q, w, cs],
            xdev(1 if w == 0 else NX - 1),
        )

    def ry(q, cs):
        dev = {"expert": ((y + q) % NY) * NZ + z, "ctx": x * 2 + cs}
        return rc(FB.at[q, cs], YB.at[q, c], rys.at[q, cs], ryv.at[q, c], dev)

    def fy(q, cs):
        dev = {"expert": ((y + q) % NY) * NZ + z, "ctx": x * 2 + cs}
        return rc(PB.at[q, 6 + cs], YF.at[q, c], fys.at[q, cs], fyv.at[q, c], dev)

    def fy_got(q, j):
        return rc(PB.at[q, 6], YF.at[q, j], fys.at[q, 0], fyv.at[q, j], partner)

    def ry_got(q, j):
        return rc(FB.at[q, 0], YB.at[q, j], rys.at[q, 0], ryv.at[q, j], partner)

    def step_d(q):
        for k in range(3):
            for cs in range(2):
                xw(q, cs, 0, k).wait_recv()
                xw(q, cs, 1, k).wait_recv()

        def own_far():
            got_a(q, c, 0).wait_recv()
            got_a(q, c, 1).wait_recv()

        got_a(q, 1 - c, 0).wait_recv()
        got_a(q, 1 - c, 1).wait_recv()
        pl.when(q > 0)(own_far)
        gate_up = WV[0:2].reshape(4 * FFL, D)
        pre = lax.dot_general(RB[q, 0], gate_up, nt, preferred_element_type=F32)
        hidden = lax.dot_general(RB[q, 1], WV[2], nt, preferred_element_type=F32)
        pre_gate, pre_up = pre[:, 0 : 2 * FFL], pre[:, 2 * FFL :]
        sg = jax.nn.sigmoid(pre_gate)
        act = pre_gate * sg
        prod = act * pre_up * hidden
        hi = prod.astype(BF)
        lo = (prod - hi.astype(F32)).astype(BF)
        ones = jnp.ones((8, 2 * FFL), BF)
        score = lax.dot_general(ones, hi, nt, preferred_element_type=F32)
        score = score + lax.dot_general(ones, lo, nt, preferred_element_type=F32)
        SC[q, :, 0:R] = score[0:1]
        gpg = (hidden * pre_up * sg * (1.0 + pre_gate * (1.0 - sg))).astype(BF)
        gpu = (hidden * act).astype(BF)
        both = jnp.concatenate([gpg, gpu], axis=1)
        for f in (6, 7, 4, 2, 5, 3, 0, 1):
            weights = WV[0:2, :, f * FS : (f + 1) * FS].reshape(4 * FFL, FS)
            PB[q, f] = jnp.dot(both, weights, preferred_element_type=F32).astype(BF)
            if f >= 6:
                cs = f - 6
                pl.when((q > 0) | (c != cs))(lambda: fy(q, cs).start())
            elif f >= 2:
                rm(q, 0 if f >= 4 else 1, f % 2).start()

    def step_g(q):
        def total(cs):
            for w in range(2):
                rm(q, w, cs).wait_recv()
            near = PB[q, cs].astype(F32) + RM[q, 0, cs].astype(F32)
            return (near + RM[q, 1, cs].astype(F32)).astype(BF)

        for cs in range(2):
            FB[q, cs] = total(cs)
            pl.when((q > 0) | (c != cs))(lambda: ry(q, cs).start())

    def combine(q, rows_of, sums):
        e0 = ((NY - q) % NY) * 2
        for j in range(2):
            for d in range(NZ):
                pick = PLB[e0 + j, :, d * TOK : (d + 1) * TOK].astype(F32)
                weight = WT[e0 + j, :, d * TOK : (d + 1) * TOK]
                pick = pick * jnp.broadcast_to(weight, (R, TOK))
                sums[d] += lax.dot_general(
                    pick.astype(BF), rows_of[q, j], tn, preferred_element_type=F32
                )

    def step_h(q):
        for j in range(2):
            pl.when((q > 0) | (c != j))(lambda: ry_got(q, j).wait_recv())

        @pl.when(q == 0)
        def _():
            YB[0, c] = FB[0, c]

        combine(q, YB, T)

    def step_hf(q):
        for j in range(2):
            pl.when((q > 0) | (c != j))(lambda: fy_got(q, j).wait_recv())

        @pl.when(q == 0)
        def _():
            YF[0, c] = PB[0, 6 + c]

        combine(q, YF, TF)

    def scx(k):
        return rc(SC, SCR.at[me_c], scs.at[k - 1], scv.at[k - 1], cdev(k))

    def scy(k):
        return rc(SCT, YSC.at[k - 1], sys_.at[k - 1], syv.at[k - 1], ydev(NY - k))

    def scz(k):
        return rc(SE.at[k], ZSC.at[NZ - k], szs.at[k - 1], szv.at[k - 1], zdev(k))

    hf = FS // 2

    class Ring:
        def __init__(self, sums, sent, came, ss, rs):
            self.sums, self.sent, self.came, self.ss, self.rs = sums, sent, came, ss, rs

        def copy(self, way, s, p):
            lanes = pl.ds(p * hf, hf)
            return rc(
                self.sent.at[way, s - 1, :, lanes], self.came.at[way, s - 1, :, lanes],
                self.ss.at[way, s - 1, p], self.rs.at[way, s - 1, p],
                zdev(1 if way == 0 else NZ - 1),
            )

        def hop(self, way, s, p):
            d = half - (s - 1) if way == 0 else half + (s - 1)
            lanes = slice(p * hf, (p + 1) * hf)
            value = self.sums[POS[d], :, lanes]
            if s > 2 or (s == 2 and p == way):
                self.copy(way, s - 1, p).wait_recv()
                value = value + self.came[way, s - 2, :, lanes].astype(F32)
            self.sent[way, s - 1, :, lanes] = value.astype(BF)
            self.copy(way, s, p).start()

        def begin(self):
            for way in range(2):
                self.hop(way, 1, way)
            for way in range(2):
                self.hop(way, 2, 1 - way)

        def step(self, s):
            for way in range(2):
                self.hop(way, s, way)
            if s > 2:
                for way in range(2):
                    self.hop(way, s, 1 - way)

        def result(self, p):
            lanes = slice(p * hf, (p + 1) * hf)
            value = self.sums[0, :, lanes]
            for way in range(2):
                self.copy(way, half, p).wait_recv()
                value = value + self.came[way, half - 1, :, lanes].astype(F32)
            return value

    near_ring = Ring(T, ZS, ZR, zrs, zrv)
    far_ring = Ring(TF, ZSF, ZRF, fzs, fzv)

    def swap():
        return rc(OS, OR, os_, ov, xdev(2))

    pl.loop(0, Q)(step_d)
    for k in range(1, NF):
        scx(k).start()
    pl.loop(0, Q)(step_hf)
    far_ring.begin()
    step_g(0)
    far_ring.step(2)
    step_g(1)
    far_ring.step(3)
    step_g(2)
    far_ring.step(4)

    SCR[me_c] = SC[...]
    for k in range(1, NF):
        scx(k).wait_recv()
    for j in range(2):
        total = SCR[j]
        for k in range(1, NX):
            total = total + SCR[2 * k + j]
        SCT[j] = total
    for k in range(1, NY):
        scy(k).start()

    step_g(3)
    pl.loop(0, Q - 1)(step_h)
    for p in range(2):
        OS[:, p * hf : (p + 1) * hf] = far_ring.result(p).astype(BF)
    swap().start()
    step_h(Q - 1)
    near_ring.begin()
    near_ring.step(2)
    for dy in range(NY):
        if dy:
            scy(dy).wait_recv()
        for j in range(2):
            e = dy * 2 + j
            row = (NY - dy) % NY
            table = SCT[j, row, :, 0:R] if dy == 0 else YSC[dy - 1, j, row, :, 0:R]
            table = jnp.broadcast_to(table, (8, R))
            hi = table.astype(BF)
            lo = (table - hi.astype(F32)).astype(BF)
            spread = jnp.dot(hi, PLB[e], preferred_element_type=F32)
            spread = spread + jnp.dot(lo, PLB[e], preferred_element_type=F32)
            for d in range(NZ):
                SE[d, e : e + 1, :] = spread[0:1, POS[d] * TOK : (POS[d] + 1) * TOK]
    for k in range(1, NZ):
        scz(k).start()
    for s in range(3, half + 1):
        near_ring.step(s)

    gates = jnp.zeros((TOP, TOK), F32)
    ids = MB[0, 0:TOP, :]
    for d in range(NZ):
        if d:
            scz(NZ - d).wait_recv()
        piece = SE[0] if d == 0 else ZSC[d]
        for i in range(8):
            who = (2 * (((y + i // 2) % NY) * NZ + (z + d) % NZ) + i % 2).astype(F32)
            gates = gates + jnp.where(
                ids == who, jnp.broadcast_to(piece[i : i + 1, :], (TOP, TOK)), 0.0
            )
    gg[...] = gates.astype(BF)

    swap().wait_recv()
    for p in range(2):
        lanes = slice(p * hf, (p + 1) * hf)
        out[:, lanes] = (near_ring.result(p) + OR[:, lanes].astype(F32)).astype(BF)

    for m in range(3):
        for f in range(NF):
            wgive(m, f).wait_send()
    for a in range(2):
        xa(a).wait_send()
    for s in range(1, half + 1):
        for way in range(2):
            if s < half or way == 0:
                zm(way, s).wait_send()
            for a in range(2):
                if s < half or a == way:
                    zx(way, s, a).wait_send()
                    za(way, s, a).wait_send()
                if s > 1 or a == way:
                    near_ring.copy(way, s, a).wait_send()
                    far_ring.copy(way, s, a).wait_send()

    @pl.loop(0, Q)
    def _(q):
        for w in range(2):
            for cs in range(2):
                for k in range(3):
                    xw(q, cs, w, k).wait_send()
                rm(q, w, cs).wait_send()
        for cs in range(2):
            pl.when((q > 0) | (c != cs))(lambda: ry(q, cs).wait_send())
            pl.when((q > 0) | (c != cs))(lambda: fy(q, cs).wait_send())

    swap().wait_send()
    for k in range(3):
        pc(k).wait_send()
    for k in range(2):
        pa(k).wait_send()

    @pl.loop(1, U)
    def _(u):
        for k in range(3):
            yc(u, k).wait_send()
        for k in range(2):
            ya(u, k).wait_send()

    for k in range(1, NF):
        scx(k).wait_send()
    for k in range(1, NY):
        scy(k).wait_send()
    for k in range(1, NZ):
        scz(k).wait_send()


def body(tokens, grad_out, expert_ids, gate_probs, gate_weight, up_weight, down_weight):
    V, S = pltpu.VMEM, pltpu.SemaphoreType.DMA
    scratch = [
        V((NZ, 2, TOK, FS), BF), V((NZ, 2, TOK, FS), BF), V((NZ, 2 * TOP, TOK), F32),
        V((8, 1, NZ * TOK), F32), V((8, 1, NZ * TOK), F32), V((8, R, NZ * TOK), BF),
        V((U, 2, R, FS), BF), V((U, 2, R, FS), BF), V((Q, 2, R, D), BF), V((3, 2 * FFL, D), BF),
        V((Q, NF, R, FS), BF), V((Q, 2, 2, R, FS), BF),
        V((Q, 2, R, FS), BF), V((Q, 2, R, FS), BF), V((Q, 2, R, FS), BF),
        V((NZ, TOK, FS), F32), V((NZ, TOK, FS), F32),
        V((2, NZ // 2, TOK, FS), BF), V((2, NZ // 2, TOK, FS), BF),
        V((2, NZ // 2, TOK, FS), BF), V((2, NZ // 2, TOK, FS), BF),
        V((TOK, FS), BF), V((TOK, FS), BF),
        V((Q, 1, 256), F32), V((NF, Q, 1, 256), F32), V((2, Q, 1, 256), F32),
        V((NY - 1, 2, Q, 1, 256), F32), V((NZ, 8, TOK), F32), V((NZ, 8, TOK), F32),
        S((2,)), S((3, NF)), S((3, NF)), S((3, NF)),
        S((2, 4, 2)), S((2, 4, 2)), S((2, 4, 2)), S((2, 4, 2)), S((2,)), S((2,)),
        S((2, 4)), S((2, 4)), S((3, U)), S((3, Q, 2)), S((2, U)), S((2, Q, 2)),
        S((3, Q, 2, 2)), S((3, Q, 2, 2)),
        S((Q, 2)), S((Q, 2)), S((Q, 2, 2)), S((Q, 2, 2)), S((Q, 2)), S((Q, 2)),
        S((2, 4, 2)), S((2, 4, 2)), S((2, 4, 2)), S((2, 4, 2)), S(()), S(()),
        S((NF - 1,)), S((NF - 1,)), S((NY - 1,)), S((NY - 1,)), S((NZ - 1,)), S((NZ - 1,)),
    ]
    anyspec = pl.BlockSpec(memory_space=pl.ANY)
    vmem = pl.BlockSpec(memory_space=pltpu.VMEM)
    out, gates = pl.pallas_call(
        kernel,
        out_shape=(
            jax.ShapeDtypeStruct((TOK, FS), BF),
            jax.ShapeDtypeStruct((TOP, TOK), BF),
        ),
        in_specs=[anyspec] * 2 + [vmem] * 2 + [anyspec] * 3,
        out_specs=(vmem, vmem),
        scratch_shapes=scratch,
        compiler_params=pltpu.CompilerParams(
            collective_id=0, has_side_effects=True, vmem_limit_bytes=60 * 1024 * 1024
        ),
        name="expert_grad",
    )(tokens, grad_out, expert_ids.T, gate_probs.T, gate_weight, up_weight, down_weight)
    return out, gates.T


def solution(mesh):
    in_specs = (
        P("expert", "ctx"),
        P("expert", "ctx"),
        P("expert", None),
        P("expert", None),
        P("expert", "ctx", None),
        P("expert", "ctx", None),
        P("expert", "ctx", None),
    )
    out_specs = (P("expert", "ctx"), P("expert", None))
    return jax.shard_map(body, mesh=mesh, in_specs=in_specs, out_specs=out_specs, check_vma=False)
```

time: 160 us -> 138 us (0.86)
  Pallas kernels: 156 us -> 133 us
    pallas_call x1, Pallas kernels: 156 us -> 133 us  [body(): pl.pallas_call(kernel, out_shape=(jax.ShapeDtypeStruct((TOK, FS), BF), ja...]
where the time goes in v4:
time: 138 us; the launch traced here: 136 us
  Pallas kernels  133 us (96%)
  local copies, waits for them, and re-layouts  2.83 us (2%)
    pallas_call x1, Pallas kernels, body(): pl.pallas_call(kernel, out_shape=(jax.ShapeDtypeStruct((TOK, FS), BF), ja...  133 us
    unnamed x2, local copies, waits for them, and re-layouts  2.83 us

profile of v4, /device:TPU:32, one launch (start us, length us, event | category | flops | bytes accessed | tf_op | source)
XLA Modules:
  0.0 136.3 jit_solution(16904723692916852462)
XLA Ops:
  0.6 132.9 %expert_grad.1 = (bf16[128,512]{1,0:T(8,128)(2,1)}, bf16[8,128]{1,0:T(8,128)(2,1)}) custom-call(bf16[128,512]{1,0:T(8,128)(2,1)} %tok.1, bf16[128,512]{1,0:T(8,128)(2,1)} %grad.1, s32[8,128]{1,0:T(8,128)} %bitcast.3, f32[8,128]{1,0:T(8,128)} %bitcast.4, bf16[2,192,4096]{2,1,0:T(8,128)(2,1)} %wg.1, bf16[2,192,4096]{2,1,0:T(8,128)(2,1)} %wu.1, ...), custom_call_target="tpu_custom_call" | custom-call | tf_op jit(solution)/shard_map/expert_grad/pallas_call | solution.py:623
  133.5 1.6 %copy.11 = bf16[128,512]{1,0:T(8,128)(2,1)} copy(bf16[128,512]{1,0:T(8,128)(2,1)} %get-tuple-element.8) | data formatting | bytes 262144
  135.1 1.3 copy.12

commit v5 on v4

--- a/solution.py
+++ b/solution.py
@@ -365,6 +365,12 @@
         score = lax.dot_general(ones, hi, nt, preferred_element_type=F32)
         score = score + lax.dot_general(ones, lo, nt, preferred_element_type=F32)
         SC[q, :, 0:R] = score[0:1]
+
+        @pl.when(q == Q - 1)
+        def _():
+            for k in range(1, NF):
+                scx(k).start()
+
         gpg = (hidden * pre_up * sg * (1.0 + pre_gate * (1.0 - sg))).astype(BF)
         gpu = (hidden * act).astype(BF)
         both = jnp.concatenate([gpg, gpu], axis=1)
@@ -388,16 +394,19 @@
             FB[q, cs] = total(cs)
             pl.when((q > 0) | (c != cs))(lambda: ry(q, cs).start())
 
-    def combine(q, rows_of, sums):
+    def combine_slab(q, rows_of, sums, d):
         e0 = ((NY - q) % NY) * 2
         for j in range(2):
-            for d in range(NZ):
-                pick = PLB[e0 + j, :, d * TOK : (d + 1) * TOK].astype(F32)
-                weight = WT[e0 + j, :, d * TOK : (d + 1) * TOK]
-                pick = pick * jnp.broadcast_to(weight, (R, TOK))
-                sums[d] += lax.dot_general(
-                    pick.astype(BF), rows_of[q, j], tn, preferred_element_type=F32
-                )
+            pick = PLB[e0 + j, :, d * TOK : (d + 1) * TOK].astype(F32)
+            weight = WT[e0 + j, :, d * TOK : (d + 1) * TOK]
+            pick = pick * jnp.broadcast_to(weight, (R, TOK))
+            sums[d] += lax.dot_general(
+                pick.astype(BF), rows_of[q, j], tn, preferred_element_type=F32
+            )
+
+    def combine(q, rows_of, sums):
+        for d in range(NZ):
+            combine_slab(q, rows_of, sums, d)
 
     def step_h(q):
         for j in range(2):
@@ -480,17 +489,28 @@
         return rc(OS, OR, os_, ov, xdev(2))
 
     pl.loop(0, Q)(step_d)
-    for k in range(1, NF):
-        scx(k).start()
     pl.loop(0, Q)(step_hf)
     far_ring.begin()
     step_g(0)
+    step_g(1)
     far_ring.step(2)
-    step_g(1)
+    step_g(2)
     far_ring.step(3)
-    step_g(2)
+    step_g(3)
+    pl.loop(0, Q - 1)(step_h)
     far_ring.step(4)
 
+    for j in range(2):
+        ry_got(Q - 1, j).wait_recv()
+    for d in (4, 3, 5, 2, 6, 1, 7, 0):
+        combine_slab(Q - 1, YB, T, POS[d])
+        if d == half:
+            for way in range(2):
+                near_ring.hop(way, 1, way)
+        elif d == half - 1:
+            near_ring.hop(0, 2, 1)
+        elif d == half + 1:
+            near_ring.hop(1, 2, 0)
     SCR[me_c] = SC[...]
     for k in range(1, NF):
         scx(k).wait_recv()
@@ -501,15 +521,10 @@
         SCT[j] = total
     for k in range(1, NY):
         scy(k).start()
-
-    step_g(3)
-    pl.loop(0, Q - 1)(step_h)
+    near_ring.step(2)
     for p in range(2):
         OS[:, p * hf : (p + 1) * hf] = far_ring.result(p).astype(BF)
     swap().start()
-    step_h(Q - 1)
-    near_ring.begin()
-    near_ring.step(2)
     for dy in range(NY):
         if dy:
             scy(dy).wait_recv()
@@ -526,8 +541,8 @@
                 SE[d, e : e + 1, :] = spread[0:1, POS[d] * TOK : (POS[d] + 1) * TOK]
     for k in range(1, NZ):
         scz(k).start()
-    for s in range(3, half + 1):
-        near_ring.step(s)
+    near_ring.step(3)
+    near_ring.step(4)
 
     gates = jnp.zeros((TOP, TOK), F32)
     ids = MB[0, 0:TOP, :]

time: 138 us -> 135 us (0.978)
  Pallas kernels: 133 us -> 130 us
    pallas_call x1, Pallas kernels: 133 us -> 130 us  [body(): pl.pallas_call(kernel, out_shape=(jax.ShapeDtypeStruct((TOK, FS), BF), ja...]
where the time goes in v5:
time: 135 us; the launch traced here: 133 us
  Pallas kernels  130 us (96%)
  local copies, waits for them, and re-layouts  2.83 us (2%)
    pallas_call x1, Pallas kernels, body(): pl.pallas_call(kernel, out_shape=(jax.ShapeDtypeStruct((TOK, FS), BF), ja...  130 us
    unnamed x2, local copies, waits for them, and re-layouts  2.83 us

profile of v5, /device:TPU:32, one launch (start us, length us, event | category | flops | bytes accessed | tf_op | source)
XLA Modules:
  0.0 133.1 jit_solution(751448556298234266)
XLA Ops:
  0.6 129.6 %expert_grad.1 = (bf16[128,512]{1,0:T(8,128)(2,1)}, bf16[8,128]{1,0:T(8,128)(2,1)}) custom-call(bf16[128,512]{1,0:T(8,128)(2,1)} %tok.1, bf16[128,512]{1,0:T(8,128)(2,1)} %grad.1, s32[8,128]{1,0:T(8,128)} %bitcast.3, f32[8,128]{1,0:T(8,128)} %bitcast.4, bf16[2,192,4096]{2,1,0:T(8,128)(2,1)} %wg.1, bf16[2,192,4096]{2,1,0:T(8,128)(2,1)} %wu.1, ...), custom_call_target="tpu_custom_call" | custom-call | tf_op jit(solution)/shard_map/expert_grad/pallas_call | solution.py:638
  130.3 1.6 %copy.11 = bf16[128,512]{1,0:T(8,128)(2,1)} copy(bf16[128,512]{1,0:T(8,128)(2,1)} %get-tuple-element.8) | data formatting | bytes 262144
  131.9 1.3 copy.12
